TPU v7x, 768 devices: a whole 4x8x12 slice. The times are simulated.
768 devices in a mesh: dom: 96 (over z, y_lo, core), st: 8 (over y_hi, x).
Axes of the slice: x: 4, y: 8 (y_hi: 2, y_lo: 4; y = y_hi * 4 + y_lo), z: 12, core: 2. Of those that a mesh axis runs over, the one named last changes fastest.
Arguments:
- orbitals: bfloat16 [384, 196608], P('st', 'dom')
- cell_matrix: bfloat16 [512, 512], replicated
- connectivity: int32 [1536, 512], P('dom'), may hold values from 0 to 2303, as said below
- surface_nodes: int32 [96, 256], P('dom'), may hold values from 0 to 2047, as said below
- cell_scale: float32 [1536], P('dom'), may hold values from 0.3 to 3
- potential: float32 [196608], P('dom'), may hold values from -1 to 2
Outputs:
- rotated_states: bfloat16 [384, 196608], P('st', 'dom')
Inputs may be any that keep to these rules, and one draw needn't show every extreme that they name: `connectivity`: within a cell all 512 numbers differ. In each domain the first 12 cells name only the domain's own nodes (numbers below 2048); the others may also name the 256 shared-surface nodes of the next domain. `surface_nodes`: each row names 256 different nodes.
All inputs are finite; a program needn't handle non-finite values.
Results may differ from a plain program's by a relative error of at most 0.002.
The roundings to bfloat16 on the way count: a program that leaves them out, or rounds other values in their place, can miss the bound.
Values may be sent and summed in bfloat16 or wider, within the bound.
No kernel may reach another device: no remote copies, remote signals or barrier semaphores. Data moves between devices by JAX's collectives and lax.ppermute only.
A program may use at most 32 MiB of HBM per device.

v0:
```python
import jax
import jax.numpy as jnp
from jax import lax
from jax.sharding import PartitionSpec as P

DEGREE = 3
ROOT_ITERS = 4


center = 7.0
half_width = 6.0
epsilon = 1e-06


def from_behind(block, axis, distance):
    devices = range(lax.axis_size(axis))
    route = [(i - distance, i) for i in devices if i - distance in devices]
    return lax.ppermute(block, axis, route)


def apply_hamiltonian(values, connectivity, surface_ids, cell_scale, potential, cell_matrix):
    nodes_dev = values.shape[1]
    boundary = values[:, surface_ids]
    ghosts = from_behind(boundary, "dom", -1)
    extended = jnp.concatenate([values, ghosts], axis=1)
    gathered = extended[:, connectivity]
    products = jnp.dot(
        gathered.reshape(-1, gathered.shape[2]), cell_matrix, preferred_element_type=jnp.float32
    )
    products = products.reshape(gathered.shape) * cell_scale[None, :, None]
    totals = jnp.zeros(extended.shape, jnp.float32).at[:, connectivity].add(products)
    returned = from_behind(totals[:, nodes_dev:], "dom", 1)
    owned = totals[:, :nodes_dev].at[:, surface_ids].add(returned)
    return owned + potential[None, :] * values.astype(jnp.float32)


def newton_root(gram):
    highest = lax.Precision.HIGHEST
    states_all = gram.shape[0]
    scale_sum = jnp.sqrt(jnp.sum(gram * gram)) + epsilon
    identity = jnp.eye(states_all, dtype=jnp.float32)
    growing = gram / scale_sum
    inverse = identity
    for iteration in range(ROOT_ITERS):
        factor = 1.5 * identity - 0.5 * jnp.dot(inverse, growing, precision=highest)
        growing = jnp.dot(growing, factor, precision=highest)
        inverse = jnp.dot(factor, inverse, precision=highest)
    return (inverse, scale_sum)


def body(orbitals, cell_matrix, connectivity, surface_nodes, cell_scale, potential):
    surface_ids = surface_nodes[0]
    older = orbitals
    newest = orbitals
    for degree_step in range(DEGREE):
        image = apply_hamiltonian(
            newest, connectivity, surface_ids, cell_scale, potential, cell_matrix
        )
        shifted = (image - center * newest.astype(jnp.float32)) / half_width
        if degree_step == 0:
            fresh = shifted
        else:
            fresh = 2.0 * shifted - older.astype(jnp.float32)
        older = newest
        newest = fresh.astype(jnp.bfloat16)
    slabs = lax.all_to_all(newest, "st", split_axis=1, concat_axis=0, tiled=True)
    gram_part = jnp.dot(slabs, slabs.T, preferred_element_type=jnp.float32)
    gram = lax.psum(gram_part, ("dom", "st"))
    inverse, scale_sum = newton_root(gram)
    node_total = lax.axis_size("dom") * orbitals.shape[1]
    rotation = (inverse * jnp.sqrt(node_total / scale_sum)).astype(jnp.bfloat16)
    rotated = jnp.dot(rotation.T, slabs, preferred_element_type=jnp.float32).astype(jnp.bfloat16)
    return lax.all_to_all(rotated, "st", split_axis=0, concat_axis=1, tiled=True)


def solution(mesh):
    return jax.shard_map(
        body,
        mesh=mesh,
        in_specs=(P("st", "dom"), P(), P("dom", None), P("dom", None), P("dom"), P("dom")),
        out_specs=P("st", "dom"),
        check_vma=False,
    )
```

profile of v0, /device:TPU:1, one launch (start us, length us, event | category | flops | bytes accessed | tf_op | source)
XLA Modules:
  0.0 843.6 jit_solution(14445651311839209964)
XLA Ops:
  9.4 12.4 %collective-permute-start = (bf16[48,256]{0,1:T(8,128)(2,1)S(1)}, bf16[48,256]{0,1:T(8,128)(2,1)S(1)}, u32[]{:S(2)}, u32[]{:S(2)}) collective-permute-start(bf16[48,256]{0,1:T(8,128)(2,1)S(1)} %bitcast.91), channel_id=1, source_target_pairs={{8,0},{16,8},{24,16},{32,24},{40,32},{48,40},{56,48},{64,56},{72,6... | collective-permute-start | bytes 73736 | tf_op jit(solution)/shard_map/ppermute | solution.py:18
  22.7 29.2 %gather_fusion.1 = bf16[8192,48]{1,0:T(8,128)(2,1)} fusion(bf16[48,2304]{0,1:T(8,128)(2,1)S(1)} %pad_maximum_fusion, s32[8192]{0:T(1024)S(1)} %broadcast_clamp_fusion), kind=kCustom, calls=%fused_computation.1 | custom fusion | bytes 1605632 | tf_op jit(solution)/shard_map/gather | solution.py:26
  52.0 2.4 copy.48
  55.0 2.7 copy.57
  57.7 44.6 %scatter_custom_fusion = f32[48,2304]{0,1:T(8,128)S(1)} fusion(s32[8192]{0:T(1024)S(1)} %bitcast.88, f32[8192,48]{1,0:T(8,128)} %bitcast.77, f32[]{:T(128)} %constant.12.clone.1), kind=kCustom, calls=%fused_computation.57 | custom fusion | flops 393216 | bytes 442880 | tf_op jit(solution)/shard_map/scatter-add | solution.py:31
  102.3 1.9 collective-permute-start.1
  106.2 2.3 scatter_custom_fusion.1
  111.5 4.4 collective-permute-done.2
  115.9 29.2 %gather_fusion.3 = bf16[8192,48]{1,0:T(8,128)(2,1)} fusion(bf16[48,2304]{0,1:T(8,128)(2,1)S(1)} %pad_maximum_fusion.1, s32[8192]{0:T(1024)S(1)} %broadcast_clamp_fusion), kind=kCustom, calls=%fused_computation.3 | custom fusion | bytes 1605632 | tf_op jit(solution)/shard_map/gather | solution.py:26
  145.2 3.2 copy.51
  150.1 2.7 copy.58
  152.7 44.6 %scatter_custom_fusion.2 = f32[48,2304]{0,1:T(8,128)S(1)} fusion(s32[8192]{0:T(1024)S(1)} %bitcast.89, f32[8192,48]{1,0:T(8,128)} %bitcast.78, f32[]{:T(128)} %constant.12.clone.1), kind=kCustom, calls=%fused_computation.55 | custom fusion | flops 393216 | bytes 442880 | tf_op jit(solution)/shard_map/scatter-add | solution.py:31
  197.4 2.1 collective-permute-start.3
  201.2 4.0 scatter_custom_fusion.3
  207.5 2.0 collective-permute-start.4
  209.5 4.3 collective-permute-done.4
  213.9 29.2 %gather_fusion.5 = bf16[8192,48]{1,0:T(8,128)(2,1)} fusion(bf16[48,2304]{0,1:T(8,128)(2,1)S(1)} %pad_maximum_fusion.2, s32[8192]{0:T(1024)S(1)} %broadcast_clamp_fusion), kind=kCustom, calls=%fused_computation.5 | custom fusion | bytes 1605632 | tf_op jit(solution)/shard_map/gather | solution.py:26
  243.2 2.4 copy.53
  247.3 3.7 copy.59
  251.0 44.6 %scatter_custom_fusion.4 = f32[48,2304]{0,1:T(8,128)S(1)} fusion(s32[8192]{0:T(1024)S(1)} %bitcast.90, f32[8192,48]{1,0:T(8,128)} %bitcast.76, f32[]{:T(128)} %constant.12.clone.1), kind=kCustom, calls=%fused_computation.53 | custom fusion | flops 393216 | bytes 442880 | tf_op jit(solution)/shard_map/scatter-add | solution.py:31
  299.5 4.0 scatter_custom_fusion.5
  305.1 12.2 %all_to_all.38 = bf16[48,8,256]{2,0,1:T(8,128)(2,1)S(1)} all-to-all(bf16[48,8,256]{2,0,1:T(8,128)(2,1)S(1)} %copy.55), channel_id=1, replica_groups=mesh['dom'=96,'st'=8] {'st'}, dimensions={1} | all-to-all | bytes 393216 | tf_op jit(solution)/shard_map/all_to_all | solution.py:66
  318.4 483.2 %all-reduce.2.cloned.1.call-done = f32[384,384]{1,0:T(8,128)} async-done(((f32[384,384]{1,0:T(8,128)}), f32[384,384]{1,0:T(8,128)}) %all-reduce.2.cloned.1.call-update) | async-done | bytes 589840 | tf_op jit(solution)/shard_map/psum | solution.py:68
  818.6 17.4 %all_to_all.39 = bf16[8,48,256]{2,1,0:T(8,128)(2,1)S(1)} all-to-all(bf16[8,48,256]{2,1,0:T(8,128)(2,1)S(1)} %bitcast.86), channel_id=1, replica_groups=mesh['dom'=96,'st'=8] {'st'}, dimensions={0} | all-to-all | bytes 393216 | tf_op jit(solution)/shard_map/all_to_all | solution.py:73
  (56 shorter events, 40.4 us)
Async XLA Ops:
  6.5 47.9 %copy-start = (bf16[512,512]{1,0:T(8,128)(2,1)S(1)}, bf16[512,512]{1,0:T(8,128)(2,1)}, u32[]{:S(2)}) copy-start(bf16[512,512]{1,0:T(8,128)(2,1)} %param.7) | copy-start | bytes 1572868
  6.5 795.1 %all-reduce.2.cloned.1.call-start = ((), (), s32[]{:S(2)}) async-start(), calls=%async_computation.2 | async-start | bytes 1179648 | tf_op jit(solution)/shard_map/psum | solution.py:68
  9.4 13.3 %collective-permute-start = (bf16[48,256]{0,1:T(8,128)(2,1)S(1)}, bf16[48,256]{0,1:T(8,128)(2,1)S(1)}, u32[]{:S(2)}, u32[]{:S(2)}) collective-permute-start(bf16[48,256]{0,1:T(8,128)(2,1)S(1)} %bitcast.91), channel_id=1, source_target_pairs={{8,0},{16,8},{24,16},{32,24},{40,32},{48,40},{56,48},{64,56},{72,6... | collective-permute-start | bytes 73736 | tf_op jit(solution)/shard_map/ppermute | solution.py:18
  52.0 2.4 copy-start.3
  55.0 49.3 %copy-start.2 = (f32[2048]{0:T(1024)S(1)}, f32[2048]{0:T(1024)}, u32[]{:S(2)}) copy-start(f32[2048]{0:T(1024)} %param.11) | copy-start | bytes 24580
  102.3 3.9 collective-permute-start.1
  109.5 6.3 collective-permute-start.2
  197.4 3.9 collective-permute-start.3
  207.5 6.3 collective-permute-start.4
  295.6 3.9 collective-permute-start.5
  804.1 2.6 copy-start.1
Sparse Core Ops, SparseCore 0:
  318.6 483.0 all-reduce.1
where the time goes:
time: 845 us; the launch traced here: 844 us
  waiting for transfers between devices  495 us (59%)
  other arithmetic  154 us (18%)
  local copies, waits for them, and re-layouts  109 us (13%)
  blocking collectives  29.6 us (4%)
  starting transfers between devices  22.2 us (3%)
  matrix products  19.4 us (2%)
  between operations  14.5 us (2%)
    psum x1, waiting for transfers between devices, body(): gram = lax.psum(gram_part, ('dom', 'st'))  483 us
    scatter-add x3, other arithmetic, apply_hamiltonian(): jnp.zeros(extended.shape, jnp.float32).at[:, connectivity].add(products)  134 us
    gather x6, local copies, waits for them, and re-layouts, apply_hamiltonian(): gathered = extended[:, connectivity]  95.7 us
    ppermute x6, starting transfers between devices, from_behind(): return lax.ppermute(block, axis, route)  22.2 us
    all_to_all x1, blocking collectives, body(): lax.all_to_all(rotated, 'st', split_axis=0, concat_axis=1, tiled=True)  17.4 us
  transfers between devices with their start and end apart: 7, of which 7 were waited for; matrix products, arithmetic and copies ran while one was open for 0% of the time, Pallas kernels for 0%

commit v1 on v0

v1 whole, which is shorter than its diff:
```python
import functools
import jax
import jax.numpy as jnp
from jax import lax
from jax.experimental import pallas as pl
from jax.experimental.pallas import tpu as pltpu
from jax.sharding import Mesh
from jax.sharding import PartitionSpec as P

DEGREE = 3
ROOT_ITERS = 4
LOW = 256


center = 7.0
half_width = 6.0
epsilon = 1e-06


def tile_rows(row, rows):
    return jnp.broadcast_to(row, (rows, row.shape[1]))


def one_hot(low16):
    base = lax.broadcasted_iota(jnp.int32, low16.shape, 0)
    pieces = []
    for start in range(0, LOW, low16.shape[0]):
        ids = (base + start).astype(jnp.float32).astype(jnp.bfloat16)
        pieces.append(jnp.where(low16 == ids, jnp.bfloat16(1), jnp.bfloat16(0)))
    return jnp.concatenate(pieces, axis=0)


def pick_block(high, blocks):
    level, bit = list(blocks), 0
    while len(level) > 1:
        mask = (high >> bit) & 1 == 1
        nxt = []
        for i in range(0, len(level) - 1, 2):
            nxt.append(jnp.where(mask, level[i + 1], level[i]))
        if len(level) % 2:
            nxt.append(level[-1])
        level, bit = nxt, bit + 1
    return level[0]


def cells_body(n_add, first, count, n_blocks, scale_ref, *refs):
    conn_ref, matrix_ref = refs[0], refs[1]
    srcs = refs[2 : 2 + (2 if n_blocks > 8 else 1)]
    pos = 2 + len(srcs)
    adds = refs[pos : pos + n_add]
    out_ref, oh_ref, got_ref = refs[pos + n_add :][:3]
    states = srcs[0].shape[0]
    width = conn_ref.shape[1]
    columns = [srcs[0][:, b * LOW : (b + 1) * LOW] for b in range(srcs[0].shape[1] // LOW)]
    if n_blocks > 8:
        columns.append(srcs[1][...])
    stacked = jnp.concatenate(columns, axis=0)
    for i in range(count):
        row = conn_ref[first + i : first + i + 1, :]
        low16 = tile_rows(row & (LOW - 1), 16).astype(jnp.float32).astype(jnp.bfloat16)
        hot = one_hot(low16)
        oh_ref[i] = hot
        high = tile_rows(row >> 8, states)
        wide = jnp.dot(stacked, hot, preferred_element_type=jnp.float32)
        blocks = [wide[b * states : (b + 1) * states] for b in range(n_blocks)]
        got_ref[i * states : (i + 1) * states, :] = pick_block(high, blocks).astype(jnp.bfloat16)
    lefts = []
    for i in range(count):
        product = jnp.dot(
            got_ref[i * states : (i + 1) * states, :], matrix_ref[...], preferred_element_type=jnp.float32
        )
        product = product * scale_ref[first + i]
        upper = product.astype(jnp.bfloat16)
        lower = (product - upper.astype(jnp.float32)).astype(jnp.bfloat16)
        row = conn_ref[first + i : first + i + 1, :]
        high16 = tile_rows(row >> 8, states).astype(jnp.float32).astype(jnp.bfloat16)
        zero = jnp.zeros_like(upper)
        masks = [high16 == jnp.bfloat16(b) for b in range(n_blocks)]
        lefts.append(jnp.concatenate([jnp.where(m, part, zero) for part in (upper, lower) for m in masks], axis=0))
    left = jnp.concatenate(lefts, axis=1)
    right = jnp.concatenate([oh_ref[i] for i in range(count)], axis=1)
    total = lax.dot_general(left, right, (((1,), (1,)), ((), ())), preferred_element_type=jnp.float32)
    total = total[: n_blocks * states] + total[n_blocks * states :]
    for b in range(n_blocks):
        value = total[b * states : (b + 1) * states]
        for a in adds:
            if b * LOW < a.shape[1]:
                value = value + a[:, b * LOW : (b + 1) * LOW]
        out_ref[:, b * LOW : (b + 1) * LOW] = value


def cells(first, count, scale, conn, matrix, srcs, adds=()):
    states = srcs[0].shape[0]
    n_blocks = sum(s.shape[1] for s in srcs) // LOW
    smem = pl.BlockSpec(memory_space=pltpu.SMEM)
    vmem = pl.BlockSpec(memory_space=pltpu.VMEM)
    width = conn.shape[1]
    rows = states * n_blocks
    flops = 2 * count * width * (rows * LOW * 3 + states * width)
    return pl.pallas_call(
        functools.partial(cells_body, len(adds), first, count, n_blocks),
        out_shape=jax.ShapeDtypeStruct((states, n_blocks * LOW), jnp.float32),
        in_specs=[smem] + [vmem] * (2 + len(srcs) + len(adds)),
        out_specs=vmem,
        scratch_shapes=[
            pltpu.VMEM((count, LOW, width), jnp.bfloat16),
            pltpu.VMEM((count * states, width), jnp.bfloat16),
        ],
        cost_estimate=pl.CostEstimate(flops=3 * flops, bytes_accessed=3 << 20, transcendentals=0),
        name=f"cells_{first}_{count}",
    )(scale, conn, matrix, *srcs, *adds)


def combine_body(first_step, last_step, total_ref, back_ref, surf_ref, pot_ref, new_ref, *refs):
    refs = list(refs)
    old_ref = None if first_step else refs.pop(0)
    out_ref = refs.pop(0)
    states, nodes = new_ref.shape
    n_blocks = nodes // LOW
    row = surf_ref[...]
    low16 = tile_rows(row & (LOW - 1), 16).astype(jnp.float32).astype(jnp.bfloat16)
    high16 = tile_rows(row >> 8, states).astype(jnp.float32).astype(jnp.bfloat16)
    hot = one_hot(low16)
    back = back_ref[...]
    upper = back.astype(jnp.bfloat16)
    lower = (back - upper.astype(jnp.float32)).astype(jnp.bfloat16)
    zero = jnp.zeros_like(upper)
    masks = [high16 == jnp.bfloat16(b) for b in range(n_blocks)]
    left = jnp.concatenate([jnp.where(m, part, zero) for part in (upper, lower) for m in masks], axis=0)
    added = lax.dot_general(left, hot, (((1,), (1,)), ((), ())), preferred_element_type=jnp.float32)
    added = added[: n_blocks * states] + added[n_blocks * states :]
    fresh_blocks = []
    for b in range(n_blocks):
        span = slice(b * LOW, (b + 1) * LOW)
        values = new_ref[:, span].astype(jnp.float32)
        image = total_ref[:, span] + added[b * states : (b + 1) * states]
        image = image + pot_ref[:, span] * values
        fresh = (image - center * values) / half_width
        if not first_step:
            fresh = 2.0 * fresh - old_ref[:, span].astype(jnp.float32)
        fresh = fresh.astype(jnp.bfloat16)
        out_ref[:, span] = fresh
        fresh_blocks.append(fresh)
    if not last_step:
        refs.pop(0)[...] = edge_values(row, hot, fresh_blocks)


def edge_values(row, hot, columns):
    states = columns[0].shape[0]
    wide = jnp.dot(jnp.concatenate(columns, axis=0), hot, preferred_element_type=jnp.float32)
    blocks = [wide[b * states : (b + 1) * states] for b in range(len(columns))]
    return pick_block(tile_rows(row >> 8, states), blocks).astype(jnp.bfloat16)


def combine(total, back, surf, pot, newest, older, last_step):
    first_step = older is None
    states, nodes = newest.shape
    edge = surf.shape[1]
    vmem = pl.BlockSpec(memory_space=pltpu.VMEM)
    olds = () if first_step else (older,)
    outs = [jax.ShapeDtypeStruct((states, nodes), jnp.bfloat16)]
    if not last_step:
        outs.append(jax.ShapeDtypeStruct((states, edge), jnp.bfloat16))
    return pl.pallas_call(
        functools.partial(combine_body, first_step, last_step),
        out_shape=outs,
        in_specs=[vmem] * (5 + len(olds)),
        out_specs=[vmem] * len(outs),
        cost_estimate=pl.CostEstimate(flops=1 << 28, bytes_accessed=1 << 20, transcendentals=0),
        name="combine",
    )(total, back, surf, pot, newest, *olds)


def edge_body(surf_ref, new_ref, out_ref):
    row = surf_ref[...]
    low16 = tile_rows(row & (LOW - 1), 16).astype(jnp.float32).astype(jnp.bfloat16)
    columns = [new_ref[:, b * LOW : (b + 1) * LOW] for b in range(new_ref.shape[1] // LOW)]
    out_ref[...] = edge_values(row, one_hot(low16), columns)


def edge(surf, newest):
    vmem = pl.BlockSpec(memory_space=pltpu.VMEM)
    return pl.pallas_call(
        edge_body,
        out_shape=jax.ShapeDtypeStruct((newest.shape[0], surf.shape[1]), jnp.bfloat16),
        in_specs=[vmem, vmem],
        out_specs=vmem,
        name="edge",
    )(surf, newest)


def split(a):
    upper = a.astype(jnp.bfloat16)
    return upper, (a - upper.astype(jnp.float32)).astype(jnp.bfloat16)


def product(a, b):
    (ah, al), (bh, bl) = a, b
    dot = functools.partial(jnp.dot, preferred_element_type=jnp.float32)
    return dot(ah, bh) + (dot(ah, bl) + dot(al, bh))


def rotate_body(node_total, start_ref, gram_ref, field_ref, out_ref, high_ref):
    gram = gram_ref[...]
    states = gram.shape[0]
    rows = out_ref.shape[0]
    scale_sum = jnp.sqrt(jnp.sum(gram * gram, keepdims=True)) + epsilon
    eye = (
        lax.broadcasted_iota(jnp.int32, gram.shape, 0) == lax.broadcasted_iota(jnp.int32, gram.shape, 1)
    ).astype(jnp.float32)
    growing = gram / scale_sum
    factor = 1.5 * eye - 0.5 * growing
    inverse = factor
    for iteration in range(1, ROOT_ITERS):
        parts = split(factor)
        growing = product(parts, split(growing))
        if iteration > 1:
            inverse = product(split(inverse), parts)
        factor = 1.5 * eye - 0.5 * product(split(growing), split(inverse))
    high_ref[...] = inverse
    start = pl.multiple_of(start_ref[0] * rows, 16)
    mine = high_ref[pl.ds(start, rows), :]
    mine = product(split(mine), split(factor))
    turn = (mine * jnp.sqrt(node_total / scale_sum)).astype(jnp.bfloat16)
    out_ref[...] = jnp.dot(turn, field_ref[...], preferred_element_type=jnp.float32).astype(jnp.bfloat16)


def rotate(start, gram, field, rows, node_total):
    smem = pl.BlockSpec(memory_space=pltpu.SMEM)
    vmem = pl.BlockSpec(memory_space=pltpu.VMEM)
    return pl.pallas_call(
        functools.partial(rotate_body, node_total),
        out_shape=jax.ShapeDtypeStruct((rows, field.shape[1]), jnp.bfloat16),
        in_specs=[smem, vmem, vmem],
        out_specs=vmem,
        scratch_shapes=[pltpu.VMEM(gram.shape, jnp.float32)],
        name="rotate",
    )(start, gram, field)


def behind(block, distance):
    devices = range(lax.axis_size(DOM))
    route = [(i - distance, i) for i in devices if i - distance in devices]
    return lax.ppermute(block, DOM, route)


def swap(block, axes):
    return lax.all_to_all(block, axes, 0, 0, tiled=True)


def spread(block, axes):
    return swap(jnp.broadcast_to(block[None], (lax.axis_size(axes), *block.shape)), axes)


def gram_total(rows):
    states, columns = rows.shape
    depth, pairs = lax.axis_size("z"), lax.axis_size("yh")
    part = jnp.sum(swap(rows.reshape(depth, states // depth, columns), "z"), axis=0)
    parts = spread(part, ("yl", "core", "yh"))
    parts = parts.reshape(-1, pairs, *part.shape).sum(axis=0)
    whole = spread(parts, ("z", "x")).reshape(depth, -1, *parts.shape)
    return whole.transpose(1, 2, 0, 3, 4).reshape(-1, columns)


def field_all(newest):
    other = lax.ppermute(newest, "yh", [(0, 1), (1, 0)])
    first = lax.axis_index("yh") == 0
    pair = jnp.stack([jnp.where(first, newest, other), jnp.where(first, other, newest)])
    return spread(pair, "x").reshape(-1, newest.shape[1])


def body(orbitals, cell_matrix, connectivity, surface_nodes, cell_scale, potential):
    pot = potential[None, :]
    cell_args = (cell_scale, connectivity, cell_matrix)
    cell_count = connectivity.shape[0]
    inner = cell_count - cell_count // 4
    half = inner // 2
    older, newest = None, orbitals
    boundary = edge(surface_nodes, newest)
    for degree_step in range(DEGREE):
        last = degree_step == DEGREE - 1
        ghosts = behind(boundary, -1)
        first_total = cells(0, half, *cell_args, (newest,))
        shared = cells(inner, cell_count - inner, *cell_args, (newest, ghosts))
        returned = behind(shared[:, newest.shape[1]:], 1)
        total = cells(half, inner - half, *cell_args, (newest,), (first_total, shared))
        result = combine(total, returned, surface_nodes, pot, newest, older, last)
        older, newest = newest, result[0]
        boundary = None if last else result[1]
    field = field_all(newest)
    rows = lax.dot_general(newest, field, (((1,), (1,)), ((), ())), preferred_element_type=jnp.float32)
    node_total = lax.axis_size(DOM) * orbitals.shape[1]
    start = lax.axis_index(("x", "yh")).astype(jnp.int32)[None]
    return rotate(start, gram_total(rows), field, orbitals.shape[0], node_total)


DOM = ("z", "yl", "core")
ST = ("yh", "x")


def solution(mesh):
    dom, st = mesh.shape["dom"], mesh.shape["st"]
    fine = Mesh(mesh.devices.reshape(dom // 8, 4, 2, 2, st // 2), (*DOM, *ST))
    return jax.shard_map(
        body,
        mesh=fine,
        in_specs=(P(ST, DOM), P(), P(DOM, None), P(DOM, None), P(DOM), P(DOM)),
        out_specs=P(ST, DOM),
        check_vma=False,
    )
```

time: 845 us -> 205 us (0.24)
  waiting for transfers between devices: 495 us -> 57.5 us
  other arithmetic: 154 us -> 1.05 us
  local copies, waits for them, and re-layouts: 109 us -> 9.59 us
  Pallas kernels: 0 us -> 57.5 us
  matrix products: 19.4 us -> 0.6 us
  between operations: 14.5 us -> 0.16 us
  starting transfers between devices: 22.2 us -> 35.9 us
  blocking collectives: 29.6 us -> 41.4 us
    psum x1 -> x0, waiting for transfers between devices: 483 us -> none  [body(): gram = lax.psum(gram_part, ('dom', 'st'))]
    scatter-add x6 -> x0, other arithmetic: 144 us -> none  [the longest x3 134 us: apply_hamiltonian(): jnp.zeros(extended.shape, jnp.float32).at[:, connectivity].add(products)]
    gather x9 -> x0, local copies, waits for them, and re-layouts: 98.3 us -> none  [the longest x6 95.7 us: apply_hamiltonian(): gathered = extended[:, connectivity]]
    pallas_call x0 -> x14, Pallas kernels: none -> 57.5 us  [the longest x9 40.4 us: cells(): pl.pallas_call(functools.partial(cells_body, len(adds), first, count, n_b...]
    all_to_all x0 -> x2, waiting for transfers between devices: none -> 46.2 us  [swap(): return lax.all_to_all(block, axes, 0, 0, tiled=True)]
    dot_general x16 -> x1, matrix products: 19.4 us -> 0.6 us  [body(): lax.dot_general(newest, field, (((1,), (1,)), ((), ())), preferred_elemen...]
    all_to_all x2, blocking collectives: 29.6 us -> 41.4 us  [swap(): return lax.all_to_all(block, axes, 0, 0, tiled=True)]
    mul x3 -> x0, local copies, waits for them, and re-layouts: 9.05 us -> none  [apply_hamiltonian(): products = products.reshape(gathered.shape) * cell_scale[None, :, None]]
  transfers between devices with their start and end apart: 7 -> 9, of which waited for: 7 -> 3; matrix products, arithmetic and copies ran while one was open for 0% -> 0% of each run, Pallas kernels for 0% -> 14%
where the time goes in v1:
time: 205 us; the launch traced here: 204 us
  Pallas kernels  57.5 us (28%)
  waiting for transfers between devices  57.5 us (28%)
  blocking collectives  41.4 us (20%)
  starting transfers between devices  35.9 us (18%)
  local copies, waits for them, and re-layouts  9.59 us (5%)
    all_to_all x2, waiting for transfers between devices, swap(): return lax.all_to_all(block, axes, 0, 0, tiled=True)  46.2 us
    all_to_all x2, blocking collectives, swap(): return lax.all_to_all(block, axes, 0, 0, tiled=True)  41.4 us
    pallas_call x9, Pallas kernels, cells(): pl.pallas_call(functools.partial(cells_body, len(adds), first, count, n_b...  40.4 us
    ppermute x6, starting transfers between devices, behind(): return lax.ppermute(block, DOM, route)  25.5 us
    ppermute x1, waiting for transfers between devices, field_all(): other = lax.ppermute(newest, 'yh', [(0, 1), (1, 0)])  11.3 us
    pallas_call x1, Pallas kernels, rotate(): pl.pallas_call(functools.partial(rotate_body, node_total), out_shape=jax....  8.51 us
    all_to_all x2, starting transfers between devices, swap(): return lax.all_to_all(block, axes, 0, 0, tiled=True)  8.46 us
    pallas_call x3, Pallas kernels, combine(): pl.pallas_call(functools.partial(combine_body, first_step, last_step), ou...  6.83 us
  transfers between devices with their start and end apart: 9, of which 3 were waited for; matrix products, arithmetic and copies ran while one was open for 0% of the time, Pallas kernels for 14%

profile of v1, /device:TPU:1, one launch (start us, length us, event | category | flops | bytes accessed | tf_op | source)
XLA Modules:
  0.0 203.7 jit_solution(14220811410723272888)
XLA Ops:
  1.8 12.4 %collective-permute-start = (bf16[48,256]{1,0:T(8,128)(2,1)}, bf16[48,256]{1,0:T(8,128)(2,1)S(1)}, u32[]{:S(2)}, u32[]{:S(2)}) collective-permute-start(bf16[48,256]{1,0:T(8,128)(2,1)} %edge.1), channel_id=1, source_target_pairs={{8,0},{16,8},{24,16},{32,24},{40,32},{48,40},{56,48},{64,56},{72,6... | collective-permute-start | bytes 73736 | tf_op jit(solution)/shard_map/ppermute | solution.py:244
  14.1 4.6 %cells_0_6.3.refs_3_ = f32[48,2048]{1,0:T(8,128)} custom-call(f32[16]{0:T(128)} %scale_ref.17, s32[16,512]{1,0:T(8,128)} %refs_0_.19, bf16[512,512]{1,0:T(8,128)(2,1)} %refs_1_.17, bf16[48,2048]{1,0:T(8,128)(2,1)} %refs_0_.16), custom_call_target="tpu_custom_call" | custom-call | flops 5888802816 | bytes 3145728 | tf_op jit(solution)/shard_map/cells_0_6/pallas_call | solution.py:100
  19.4 3.9 %cells_12_4.3.refs_4_ = f32[48,2304]{1,0:T(8,128)} custom-call(f32[16]{0:T(128)} %scale_ref.17, s32[16,512]{1,0:T(8,128)} %refs_0_.19, bf16[512,512]{1,0:T(8,128)(2,1)} %refs_1_.17, bf16[48,2048]{1,0:T(8,128)(2,1)} %refs_0_.16, bf16[48,256]{1,0:T(8,128)(2,1)} %copy-done.7), custom_call_target="tpu_custom_call" | custom-call | flops 4378853376 | bytes 3145728 | tf_op jit(solution)/shard_map/cells_12_4/pallas_call | solution.py:100
  26.1 4.9 %cells_6_6.3.total_ref = f32[48,2048]{1,0:T(8,128)} custom-call(f32[16]{0:T(128)} %scale_ref.17, s32[16,512]{1,0:T(8,128)} %refs_0_.19, bf16[512,512]{1,0:T(8,128)(2,1)} %refs_1_.17, bf16[48,2048]{1,0:T(8,128)(2,1)} %refs_0_.16, f32[48,2048]{1,0:T(8,128)} %cells_0_6.3.refs_3_, f32[48,2304]{1,0:T(8,128)} %cells_12_4.3.refs_4_), custom_call_target="tpu_custom_call" | custom-call | flops 5888802816 | bytes 3145728 | tf_op jit(solution)/shard_map/cells_6_6/pallas_call | solution.py:100
  31.6 2.3 %combine.3 = (bf16[48,2048]{1,0:T(8,128)(2,1)}, bf16[48,256]{1,0:T(8,128)(2,1)}) custom-call(f32[48,2048]{1,0:T(8,128)} %cells_6_6.3.total_ref, f32[48,256]{1,0:T(8,128)} %copy-done.3, s32[1,256]{1,0:T(1,128)} %surf_ref.7, f32[1,2048]{1,0:T(1,128)} %bitcast.18, bf16[48,2048]{1,0:T(8,128)(2,1)} %refs_0_.16), custom_call_target="tpu_custom_call" | custom-call | flops 268435456 | bytes 1048576 | tf_op jit(solution)/shard_map/combine/pallas_call | solution.py:164
  33.8 2.4 %collective-permute-start.2 = (bf16[48,256]{1,0:T(8,128)(2,1)}, bf16[48,256]{1,0:T(8,128)(2,1)S(1)}, u32[]{:S(2)}, u32[]{:S(2)}) collective-permute-start(bf16[48,256]{1,0:T(8,128)(2,1)} %get-tuple-element.10), channel_id=1, source_target_pairs={{8,0},{16,8},{24,16},{32,24},{40,32},{48,40},{56,48},{64,56},{72,6... | collective-permute-start | bytes 73736 | tf_op jit(solution)/shard_map/ppermute | solution.py:244
  36.2 4.6 %cells_0_6.4.refs_3_ = f32[48,2048]{1,0:T(8,128)} custom-call(f32[16]{0:T(128)} %scale_ref.17, s32[16,512]{1,0:T(8,128)} %refs_0_.19, bf16[512,512]{1,0:T(8,128)(2,1)} %refs_1_.17, bf16[48,2048]{1,0:T(8,128)(2,1)} %get-tuple-element.9.refs_2_.new_ref.refs_0_), custom_call_target="tpu_custom_call" | custom-call | flops 5888802816 | bytes 3145728 | tf_op jit(solution)/shard_map/cells_0_6/pallas_call | solution.py:100
  41.4 3.9 %cells_12_4.4.refs_4_ = f32[48,2304]{1,0:T(8,128)} custom-call(f32[16]{0:T(128)} %scale_ref.17, s32[16,512]{1,0:T(8,128)} %refs_0_.19, bf16[512,512]{1,0:T(8,128)(2,1)} %refs_1_.17, bf16[48,2048]{1,0:T(8,128)(2,1)} %get-tuple-element.9.refs_2_.new_ref.refs_0_, bf16[48,256]{1,0:T(8,128)(2,1)} %copy-done.5), custom_call_target="tpu_custom_call" | custom-call | flops 4378853376 | bytes 3145728 | tf_op jit(solution)/shard_map/cells_12_4/pallas_call | solution.py:100
  46.2 3.3 %collective-permute-start.3 = (f32[48,256]{1,0:T(8,128)S(1)}, f32[48,256]{1,0:T(8,128)S(1)}, u32[]{:S(2)}, u32[]{:S(2)}) collective-permute-start(f32[48,256]{1,0:T(8,128)S(1)} %slice.13), channel_id=1, source_target_pairs={{0,8},{8,16},{16,24},{24,32},{32,40},{40,48},{48,56},{56,64},{64,7... | collective-permute-start | bytes 147464 | tf_op jit(solution)/shard_map/ppermute | solution.py:244
  49.5 4.9 %cells_6_6.4.total_ref = f32[48,2048]{1,0:T(8,128)} custom-call(f32[16]{0:T(128)} %scale_ref.17, s32[16,512]{1,0:T(8,128)} %refs_0_.19, bf16[512,512]{1,0:T(8,128)(2,1)} %refs_1_.17, bf16[48,2048]{1,0:T(8,128)(2,1)} %get-tuple-element.9.refs_2_.new_ref.refs_0_, f32[48,2048]{1,0:T(8,128)} %cells_0_6.4.refs_3_, f32[48,2304]{1,0:T(8,128)} %cells_12_4.4.refs_4_), custom_call_target="tpu_custom_call" | custom-call | flops 5888802816 | bytes 3145728 | tf_op jit(solution)/shard_map/cells_6_6/pallas_call | solution.py:100
  55.0 2.4 %combine.4 = (bf16[48,2048]{1,0:T(8,128)(2,1)}, bf16[48,256]{1,0:T(8,128)(2,1)}) custom-call(f32[48,2048]{1,0:T(8,128)} %cells_6_6.4.total_ref, f32[48,256]{1,0:T(8,128)} %copy-done.4, s32[1,256]{1,0:T(1,128)} %surf_ref.7, f32[1,2048]{1,0:T(1,128)} %bitcast.19, bf16[48,2048]{1,0:T(8,128)(2,1)} %get-tuple-element.9.refs_2_.new_ref.refs_0_, ...), custom_call_target="tpu_custom_call" | custom-call | flops 268435456 | bytes 1048576 | tf_op jit(solution)/shard_map/combine/pallas_call | solution.py:164
  59.3 4.6 %cells_0_6.5.refs_3_ = f32[48,2048]{1,0:T(8,128)} custom-call(f32[16]{0:T(128)} %scale_ref.17, s32[16,512]{1,0:T(8,128)} %refs_0_.19, bf16[512,512]{1,0:T(8,128)(2,1)} %refs_1_.17, bf16[48,2048]{1,0:T(8,128)(2,1)} %get-tuple-element.11.refs_2_.new_ref), custom_call_target="tpu_custom_call" | custom-call | flops 5888802816 | bytes 3145728 | tf_op jit(solution)/shard_map/cells_0_6/pallas_call | solution.py:100
  64.5 3.9 %cells_12_4.5.refs_4_ = f32[48,2304]{1,0:T(8,128)} custom-call(f32[16]{0:T(128)} %scale_ref.17, s32[16,512]{1,0:T(8,128)} %refs_0_.19, bf16[512,512]{1,0:T(8,128)(2,1)} %refs_1_.17, bf16[48,2048]{1,0:T(8,128)(2,1)} %get-tuple-element.11.refs_2_.new_ref, bf16[48,256]{1,0:T(8,128)(2,1)} %copy-done.6), custom_call_target="tpu_custom_call" | custom-call | flops 4378853376 | bytes 3145728 | tf_op jit(solution)/shard_map/cells_12_4/pallas_call | solution.py:100
  69.3 3.6 %collective-permute-start.5 = (f32[48,256]{1,0:T(8,128)S(1)}, f32[48,256]{1,0:T(8,128)S(1)}, u32[]{:S(2)}, u32[]{:S(2)}) collective-permute-start(f32[48,256]{1,0:T(8,128)S(1)} %slice.14), channel_id=1, source_target_pairs={{0,8},{8,16},{16,24},{24,32},{32,40},{40,48},{48,56},{56,64},{64,7... | collective-permute-start | bytes 147464 | tf_op jit(solution)/shard_map/ppermute | solution.py:244
  72.9 4.9 %cells_6_6.5.total_ref = f32[48,2048]{1,0:T(8,128)} custom-call(f32[16]{0:T(128)} %scale_ref.17, s32[16,512]{1,0:T(8,128)} %refs_0_.19, bf16[512,512]{1,0:T(8,128)(2,1)} %refs_1_.17, bf16[48,2048]{1,0:T(8,128)(2,1)} %get-tuple-element.11.refs_2_.new_ref, f32[48,2048]{1,0:T(8,128)} %cells_0_6.5.refs_3_, f32[48,2304]{1,0:T(8,128)} %cells_12_4.5.refs_4_), custom_call_target="tpu_custom_call" | custom-call | flops 5888802816 | bytes 3145728 | tf_op jit(solution)/shard_map/cells_6_6/pallas_call | solution.py:100
  78.4 2.2 %combine.5 = bf16[48,2048]{1,0:T(8,128)(2,1)} custom-call(f32[48,2048]{1,0:T(8,128)} %cells_6_6.5.total_ref, f32[48,256]{1,0:T(8,128)} %copy-done.2, s32[1,256]{1,0:T(1,128)} %surf_ref.7, f32[1,2048]{1,0:T(1,128)} %bitcast.20, bf16[48,2048]{1,0:T(8,128)(2,1)} %get-tuple-element.11.refs_2_.new_ref, bf16[48,2048]{1,0:T(8,128)(2,1)} %get-tuple-element.9.refs_2_.new_ref.refs_0_), custom_call_target="tpu_custom_call" | custom-call | flops 268435456 | bytes 1048576 | tf_op jit(solution)/shard_map/combine/pallas_call | solution.py:164
  82.6 11.3 %collective-permute-done.6 = bf16[48,2048]{1,0:T(8,128)(2,1)S(1)} collective-permute-done((bf16[48,2048]{1,0:T(8,128)(2,1)}, bf16[48,2048]{1,0:T(8,128)(2,1)S(1)}, u32[]{:S(2)}, u32[]{:S(2)}) %collective-permute-start.6) | collective-permute-done | bytes 196640 | tf_op jit(solution)/shard_map/ppermute | solution.py:266
  96.3 3.7 %all-to-all-start = ((bf16[4,2,48,2048]{3,2,1,0:T(8,128)(2,1)}), bf16[4,2,48,2048]{3,2,1,0:T(8,128)(2,1)S(1)}, u32[]{:S(2)}, u32[]{:S(2)}) async-start(bf16[4,2,48,2048]{3,2,1,0:T(8,128)(2,1)} %broadcast_in_dim.12), calls=%async_computation | async-start | bytes 3145728 | tf_op jit(solution)/shard_map/all_to_all | solution.py:248
  100.1 20.6 %all-to-all-done = bf16[4,2,48,2048]{3,2,1,0:T(8,128)(2,1)S(1)} async-done(((bf16[4,2,48,2048]{3,2,1,0:T(8,128)(2,1)}), bf16[4,2,48,2048]{3,2,1,0:T(8,128)(2,1)S(1)}, u32[]{:S(2)}, u32[]{:S(2)}) %all-to-all-start) | async-done | bytes 1572896 | tf_op jit(solution)/shard_map/all_to_all | solution.py:248
  121.3 21.0 %all_to_all.20 = f32[12,4,384]{2,1,0:T(4,128)S(1)} all-to-all(f32[12,4,384]{2,1,0:T(4,128)S(1)} %copy.17), channel_id=1, replica_groups=mesh['z'=12,'yl'=4,'core'=2,'yh'=2,'x'=4] {'z'}, dimensions={0} | all-to-all | bytes 147456 | tf_op jit(solution)/shard_map/all_to_all | solution.py:248
  142.4 20.4 %all_to_all.21 = f32[16,4,384]{2,1,0:T(4,128)S(1)} all-to-all(f32[16,4,384]{2,1,0:T(4,128)S(1)} %broadcast_in_dim.13), channel_id=1, replica_groups=mesh['z'=12,'yl'=4,'core'=2,'yh'=2,'x'=4] {'yl','core','yh'}, dimensions={0} | all-to-all | bytes 196608 | tf_op jit(solution)/shard_map/all_to_all | solution.py:248
  163.7 4.8 %all-to-all-start.3 = ((f32[48,2,4,384]{3,2,1,0:T(4,128)}), f32[48,2,4,384]{3,2,1,0:T(4,128)S(1)}, u32[]{:S(2)}, u32[]{:S(2)}) async-start(f32[48,2,4,384]{3,2,1,0:T(4,128)} %broadcast_in_dim.28), calls=%async_computation.3 | async-start | bytes 1179648 | tf_op jit(solution)/shard_map/all_to_all | solution.py:248
  168.5 25.6 %all-to-all-done.3 = f32[48,2,4,384]{3,2,1,0:T(4,128)S(1)} async-done(((f32[48,2,4,384]{3,2,1,0:T(4,128)}), f32[48,2,4,384]{3,2,1,0:T(4,128)S(1)}, u32[]{:S(2)}, u32[]{:S(2)}) %all-to-all-start.3) | async-done | bytes 589856 | tf_op jit(solution)/shard_map/all_to_all | solution.py:248
  195.2 8.5 %rotate.1 = bf16[48,2048]{1,0:T(8,128)(2,1)} custom-call(s32[1]{0:T(128)} %bitcast.start_ref, f32[384,384]{1,0:T(8,128)} %reshape.20.gram_ref, bf16[384,2048]{1,0:T(8,128)(2,1)} %bitcast.15), custom_call_target="tpu_custom_call" | custom-call | tf_op jit(solution)/shard_map/rotate/pallas_call | solution.py:231
  (41 shorter events, 18.8 us)
Async XLA Ops:
  1.8 17.0 %collective-permute-start = (bf16[48,256]{1,0:T(8,128)(2,1)}, bf16[48,256]{1,0:T(8,128)(2,1)S(1)}, u32[]{:S(2)}, u32[]{:S(2)}) collective-permute-start(bf16[48,256]{1,0:T(8,128)(2,1)} %edge.1), channel_id=1, source_target_pairs={{8,0},{16,8},{24,16},{32,24},{40,32},{48,40},{56,48},{64,56},{72,6... | collective-permute-start | bytes 73736 | tf_op jit(solution)/shard_map/ppermute | solution.py:244
  18.8 0.6 copy-start.7
  24.1 6.8 %collective-permute-start.1 = (f32[48,256]{1,0:T(8,128)S(1)}, f32[48,256]{1,0:T(8,128)S(1)}, u32[]{:S(2)}, u32[]{:S(2)}) collective-permute-start(f32[48,256]{1,0:T(8,128)S(1)} %slice.12), channel_id=1, source_target_pairs={{0,8},{8,16},{16,24},{24,32},{32,40},{40,48},{48,56},{56,64},{64,7... | collective-permute-start | bytes 147464 | tf_op jit(solution)/shard_map/ppermute | solution.py:244
  30.9 0.6 copy-start.3
  33.8 7.0 %collective-permute-start.2 = (bf16[48,256]{1,0:T(8,128)(2,1)}, bf16[48,256]{1,0:T(8,128)(2,1)S(1)}, u32[]{:S(2)}, u32[]{:S(2)}) collective-permute-start(bf16[48,256]{1,0:T(8,128)(2,1)} %get-tuple-element.10), channel_id=1, source_target_pairs={{8,0},{16,8},{24,16},{32,24},{40,32},{48,40},{56,48},{64,56},{72,6... | collective-permute-start | bytes 73736 | tf_op jit(solution)/shard_map/ppermute | solution.py:244
  40.8 0.6 copy-start.5
  46.2 8.2 %collective-permute-start.3 = (f32[48,256]{1,0:T(8,128)S(1)}, f32[48,256]{1,0:T(8,128)S(1)}, u32[]{:S(2)}, u32[]{:S(2)}) collective-permute-start(f32[48,256]{1,0:T(8,128)S(1)} %slice.13), channel_id=1, source_target_pairs={{0,8},{8,16},{16,24},{24,32},{32,40},{40,48},{48,56},{56,64},{64,7... | collective-permute-start | bytes 147464 | tf_op jit(solution)/shard_map/ppermute | solution.py:244
  54.4 0.6 copy-start.4
  57.4 6.5 %collective-permute-start.4 = (bf16[48,256]{1,0:T(8,128)(2,1)}, bf16[48,256]{1,0:T(8,128)(2,1)S(1)}, u32[]{:S(2)}, u32[]{:S(2)}) collective-permute-start(bf16[48,256]{1,0:T(8,128)(2,1)} %get-tuple-element.12), channel_id=1, source_target_pairs={{8,0},{16,8},{24,16},{32,24},{40,32},{48,40},{56,48},{64,56},{72,6... | collective-permute-start | bytes 73736 | tf_op jit(solution)/shard_map/ppermute | solution.py:244
  63.9 0.6 copy-start.6
  69.3 8.5 %collective-permute-start.5 = (f32[48,256]{1,0:T(8,128)S(1)}, f32[48,256]{1,0:T(8,128)S(1)}, u32[]{:S(2)}, u32[]{:S(2)}) collective-permute-start(f32[48,256]{1,0:T(8,128)S(1)} %slice.14), channel_id=1, source_target_pairs={{0,8},{8,16},{16,24},{24,32},{32,40},{40,48},{48,56},{56,64},{64,7... | collective-permute-start | bytes 147464 | tf_op jit(solution)/shard_map/ppermute | solution.py:244
  77.8 0.6 copy-start.2
  80.7 13.2 %collective-permute-start.6 = (bf16[48,2048]{1,0:T(8,128)(2,1)}, bf16[48,2048]{1,0:T(8,128)(2,1)S(1)}, u32[]{:S(2)}, u32[]{:S(2)}) collective-permute-start(bf16[48,2048]{1,0:T(8,128)(2,1)} %combine.5), channel_id=1, source_target_pairs={{0,4},{4,0},{1,5},{5,1},{2,6},{6,2},{3,7},{7,3},{8,12},{12,8},{9,1... | collective-permute-start | bytes 589832 | tf_op jit(solution)/shard_map/ppermute | solution.py:266
  96.3 3.7 %copy-start.1 = (bf16[48,2048]{1,0:T(8,128)(2,1)S(1)}, bf16[48,2048]{1,0:T(8,128)(2,1)}, u32[]{:S(2)}) copy-start(bf16[48,2048]{1,0:T(8,128)(2,1)} %combine.5) | copy-start | bytes 589828
  96.3 24.4 %all-to-all-start = ((bf16[4,2,48,2048]{3,2,1,0:T(8,128)(2,1)}), bf16[4,2,48,2048]{3,2,1,0:T(8,128)(2,1)S(1)}, u32[]{:S(2)}, u32[]{:S(2)}) async-start(bf16[4,2,48,2048]{3,2,1,0:T(8,128)(2,1)} %broadcast_in_dim.12), calls=%async_computation | async-start | bytes 3145728 | tf_op jit(solution)/shard_map/all_to_all | solution.py:248
  120.7 43.0 %copy-start = (bf16[4,2,48,2048]{3,2,1,0:T(8,128)(2,1)}, bf16[4,2,48,2048]{3,2,1,0:T(8,128)(2,1)S(1)}, u32[]{:S(2)}) copy-start(bf16[4,2,48,2048]{3,2,1,0:T(8,128)(2,1)S(1)} %all-to-all-done) | copy-start | bytes 4718596
  163.7 30.4 %all-to-all-start.3 = ((f32[48,2,4,384]{3,2,1,0:T(4,128)}), f32[48,2,4,384]{3,2,1,0:T(4,128)S(1)}, u32[]{:S(2)}, u32[]{:S(2)}) async-start(f32[48,2,4,384]{3,2,1,0:T(4,128)} %broadcast_in_dim.28), calls=%async_computation.3 | async-start | bytes 1179648 | tf_op jit(solution)/shard_map/all_to_all | solution.py:248

commit v2 on v1

--- a/solution.py
+++ b/solution.py
@@ -10,6 +10,7 @@
 DEGREE = 3
 ROOT_ITERS = 4
 LOW = 256
+VMEM_LIMIT = 24 << 20
 
 
 center = 7.0
@@ -48,7 +49,8 @@
     srcs = refs[2 : 2 + (2 if n_blocks > 8 else 1)]
     pos = 2 + len(srcs)
     adds = refs[pos : pos + n_add]
-    out_ref, oh_ref, got_ref = refs[pos + n_add :][:3]
+    out_refs = refs[pos + n_add : -2]
+    oh_ref, got_ref = refs[-2:]
     states = srcs[0].shape[0]
     width = conn_ref.shape[1]
     columns = [srcs[0][:, b * LOW : (b + 1) * LOW] for b in range(srcs[0].shape[1] // LOW)]
@@ -64,12 +66,10 @@
         wide = jnp.dot(stacked, hot, preferred_element_type=jnp.float32)
         blocks = [wide[b * states : (b + 1) * states] for b in range(n_blocks)]
         got_ref[i * states : (i + 1) * states, :] = pick_block(high, blocks).astype(jnp.bfloat16)
+    products = jnp.dot(got_ref[...], matrix_ref[...], preferred_element_type=jnp.float32)
     lefts = []
     for i in range(count):
-        product = jnp.dot(
-            got_ref[i * states : (i + 1) * states, :], matrix_ref[...], preferred_element_type=jnp.float32
-        )
-        product = product * scale_ref[first + i]
+        product = products[i * states : (i + 1) * states] * scale_ref[first + i]
         upper = product.astype(jnp.bfloat16)
         lower = (product - upper.astype(jnp.float32)).astype(jnp.bfloat16)
         row = conn_ref[first + i : first + i + 1, :]
@@ -86,7 +86,8 @@
         for a in adds:
             if b * LOW < a.shape[1]:
                 value = value + a[:, b * LOW : (b + 1) * LOW]
-        out_ref[:, b * LOW : (b + 1) * LOW] = value
+        out_ref, place = (out_refs[0], b) if b < 8 else (out_refs[1], 0)
+        out_ref[:, place * LOW : (place + 1) * LOW] = value
 
 
 def cells(first, count, scale, conn, matrix, srcs, adds=()):
@@ -99,19 +100,20 @@
     flops = 2 * count * width * (rows * LOW * 3 + states * width)
     return pl.pallas_call(
         functools.partial(cells_body, len(adds), first, count, n_blocks),
-        out_shape=jax.ShapeDtypeStruct((states, n_blocks * LOW), jnp.float32),
+        out_shape=[jax.ShapeDtypeStruct(s.shape, jnp.float32) for s in srcs],
         in_specs=[smem] + [vmem] * (2 + len(srcs) + len(adds)),
-        out_specs=vmem,
+        out_specs=[vmem] * len(srcs),
         scratch_shapes=[
             pltpu.VMEM((count, LOW, width), jnp.bfloat16),
             pltpu.VMEM((count * states, width), jnp.bfloat16),
         ],
         cost_estimate=pl.CostEstimate(flops=3 * flops, bytes_accessed=3 << 20, transcendentals=0),
+        compiler_params=pltpu.CompilerParams(vmem_limit_bytes=VMEM_LIMIT),
         name=f"cells_{first}_{count}",
     )(scale, conn, matrix, *srcs, *adds)
 
 
-def combine_body(first_step, last_step, total_ref, back_ref, surf_ref, pot_ref, new_ref, *refs):
+def combine_body(first_step, last_step, side_ref, total_ref, back_ref, surf_ref, pot_ref, new_ref, *refs):
     refs = list(refs)
     old_ref = None if first_step else refs.pop(0)
     out_ref = refs.pop(0)
@@ -139,10 +141,19 @@
         if not first_step:
             fresh = 2.0 * fresh - old_ref[:, span].astype(jnp.float32)
         fresh = fresh.astype(jnp.bfloat16)
-        out_ref[:, span] = fresh
+        if not last_step:
+            out_ref[:, span] = fresh
         fresh_blocks.append(fresh)
-    if not last_step:
-        refs.pop(0)[...] = edge_values(row, hot, fresh_blocks)
+    if last_step:
+        first = side_ref[0] == 0
+        middle = n_blocks // 2
+        for b in range(middle):
+            span = slice(b * LOW, (b + 1) * LOW)
+            early, late = fresh_blocks[b], fresh_blocks[middle + b]
+            out_ref[:, span] = jnp.where(first, early, late)
+            refs[0][:, span] = jnp.where(first, late, early)
+    else:
+        refs[0][...] = edge_values(row, hot, fresh_blocks)
 
 
 def edge_values(row, hot, columns):
@@ -152,23 +163,26 @@
     return pick_block(tile_rows(row >> 8, states), blocks).astype(jnp.bfloat16)
 
 
-def combine(total, back, surf, pot, newest, older, last_step):
+def combine(side, total, back, surf, pot, newest, older, last_step):
     first_step = older is None
     states, nodes = newest.shape
     edge = surf.shape[1]
     vmem = pl.BlockSpec(memory_space=pltpu.VMEM)
     olds = () if first_step else (older,)
-    outs = [jax.ShapeDtypeStruct((states, nodes), jnp.bfloat16)]
-    if not last_step:
-        outs.append(jax.ShapeDtypeStruct((states, edge), jnp.bfloat16))
+    if last_step:
+        outs = [jax.ShapeDtypeStruct((states, nodes // 2), jnp.bfloat16)] * 2
+    else:
+        outs = [jax.ShapeDtypeStruct((states, n), jnp.bfloat16) for n in (nodes, edge)]
+    smem = pl.BlockSpec(memory_space=pltpu.SMEM)
     return pl.pallas_call(
         functools.partial(combine_body, first_step, last_step),
         out_shape=outs,
-        in_specs=[vmem] * (5 + len(olds)),
+        in_specs=[smem] + [vmem] * (5 + len(olds)),
         out_specs=[vmem] * len(outs),
         cost_estimate=pl.CostEstimate(flops=1 << 28, bytes_accessed=1 << 20, transcendentals=0),
+        compiler_params=pltpu.CompilerParams(vmem_limit_bytes=VMEM_LIMIT),
         name="combine",
-    )(total, back, surf, pot, newest, *olds)
+    )(side, total, back, surf, pot, newest, *olds)
 
 
 def edge_body(surf_ref, new_ref, out_ref):
@@ -185,6 +199,7 @@
         out_shape=jax.ShapeDtypeStruct((newest.shape[0], surf.shape[1]), jnp.bfloat16),
         in_specs=[vmem, vmem],
         out_specs=vmem,
+        compiler_params=pltpu.CompilerParams(vmem_limit_bytes=VMEM_LIMIT),
         name="edge",
     )(surf, newest)
 
@@ -195,15 +210,40 @@
 
 
 def product(a, b):
-    (ah, al), (bh, bl) = a, b
+    rows = a.shape[0]
+    (ah, al), (bh, bl) = split(a), split(b)
     dot = functools.partial(jnp.dot, preferred_element_type=jnp.float32)
-    return dot(ah, bh) + (dot(ah, bl) + dot(al, bh))
-
-
-def rotate_body(node_total, start_ref, gram_ref, field_ref, out_ref, high_ref):
+    return dot(jnp.concatenate([ah, al, ah], axis=1), jnp.concatenate([bh, bh, bl], axis=0))
+
+
+def arrange_body(side_ref, keep_ref, other_ref, out_ref):
+    first = side_ref[0] == 0
+    states = keep_ref.shape[0]
+    keep, other = keep_ref[...], other_ref[...]
+    early, late = jnp.where(first, keep, other), jnp.where(first, other, keep)
+    for i in range(out_ref.shape[0]):
+        out_ref[i, :states] = early
+        out_ref[i, states:] = late
+
+
+def arrange(side, keep, other, copies):
+    smem = pl.BlockSpec(memory_space=pltpu.SMEM)
+    vmem = pl.BlockSpec(memory_space=pltpu.VMEM)
+    states, nodes = keep.shape
+    return pl.pallas_call(
+        arrange_body,
+        out_shape=jax.ShapeDtypeStruct((copies, 2 * states, nodes), jnp.bfloat16),
+        in_specs=[smem, vmem, vmem],
+        out_specs=vmem,
+        compiler_params=pltpu.CompilerParams(vmem_limit_bytes=VMEM_LIMIT),
+        name="arrange",
+    )(side, keep, other)
+
+
+def rotate_body(node_total, side_ref, gram_ref, field_ref, keep_ref, send_ref, high_ref, turned_ref):
     gram = gram_ref[...]
-    states = gram.shape[0]
-    rows = out_ref.shape[0]
+    rows = turned_ref.shape[0]
+    half = rows // 2
     scale_sum = jnp.sqrt(jnp.sum(gram * gram, keepdims=True)) + epsilon
     eye = (
         lax.broadcasted_iota(jnp.int32, gram.shape, 0) == lax.broadcasted_iota(jnp.int32, gram.shape, 1)
@@ -212,30 +252,33 @@
     factor = 1.5 * eye - 0.5 * growing
     inverse = factor
     for iteration in range(1, ROOT_ITERS):
-        parts = split(factor)
-        growing = product(parts, split(growing))
+        growing = product(factor, growing)
         if iteration > 1:
-            inverse = product(split(inverse), parts)
-        factor = 1.5 * eye - 0.5 * product(split(growing), split(inverse))
+            inverse = product(inverse, factor)
+        factor = 1.5 * eye - 0.5 * product(growing, inverse)
     high_ref[...] = inverse
-    start = pl.multiple_of(start_ref[0] * rows, 16)
-    mine = high_ref[pl.ds(start, rows), :]
-    mine = product(split(mine), split(factor))
+    mine = high_ref[pl.ds(pl.multiple_of(side_ref[1] * rows, 32), rows), :]
+    mine = product(mine, factor)
     turn = (mine * jnp.sqrt(node_total / scale_sum)).astype(jnp.bfloat16)
-    out_ref[...] = jnp.dot(turn, field_ref[...], preferred_element_type=jnp.float32).astype(jnp.bfloat16)
-
-
-def rotate(start, gram, field, rows, node_total):
+    turned_ref[...] = jnp.dot(turn, field_ref[...], preferred_element_type=jnp.float32).astype(jnp.bfloat16)
+    side = side_ref[0]
+    keep_ref[...] = turned_ref[pl.ds(pl.multiple_of(side * half, 16), half), :]
+    send_ref[...] = turned_ref[pl.ds(pl.multiple_of((1 - side) * half, 16), half), :]
+
+
+def rotate(side, gram, field, rows, node_total):
     smem = pl.BlockSpec(memory_space=pltpu.SMEM)
     vmem = pl.BlockSpec(memory_space=pltpu.VMEM)
+    nodes = field.shape[1]
     return pl.pallas_call(
         functools.partial(rotate_body, node_total),
-        out_shape=jax.ShapeDtypeStruct((rows, field.shape[1]), jnp.bfloat16),
+        out_shape=[jax.ShapeDtypeStruct((rows // 2, nodes), jnp.bfloat16)] * 2,
         in_specs=[smem, vmem, vmem],
-        out_specs=vmem,
-        scratch_shapes=[pltpu.VMEM(gram.shape, jnp.float32)],
+        out_specs=[vmem] * 2,
+        scratch_shapes=[pltpu.VMEM(gram.shape, jnp.float32), pltpu.VMEM((rows, nodes), jnp.bfloat16)],
+        compiler_params=pltpu.CompilerParams(vmem_limit_bytes=VMEM_LIMIT),
         name="rotate",
-    )(start, gram, field)
+    )(side, gram, field)
 
 
 def behind(block, distance):
@@ -254,19 +297,16 @@
 
 def gram_total(rows):
     states, columns = rows.shape
-    depth, pairs = lax.axis_size("z"), lax.axis_size("yh")
-    part = jnp.sum(swap(rows.reshape(depth, states // depth, columns), "z"), axis=0)
-    parts = spread(part, ("yl", "core", "yh"))
-    parts = parts.reshape(-1, pairs, *part.shape).sum(axis=0)
-    whole = spread(parts, ("z", "x")).reshape(depth, -1, *parts.shape)
-    return whole.transpose(1, 2, 0, 3, 4).reshape(-1, columns)
-
-
-def field_all(newest):
-    other = lax.ppermute(newest, "yh", [(0, 1), (1, 0)])
-    first = lax.axis_index("yh") == 0
-    pair = jnp.stack([jnp.where(first, newest, other), jnp.where(first, other, newest)])
-    return spread(pair, "x").reshape(-1, newest.shape[1])
+    near = ("yl", "core", "yh")
+    count = lax.axis_size(near)
+    part = jnp.sum(swap(rows.reshape(count, states // count, columns), near), axis=0)
+    part = jnp.sum(spread(part, "z"), axis=0)
+    block = spread(part, near).reshape(states, columns)
+    return spread(block, "x").reshape(-1, columns)
+
+
+def turn_over(block):
+    return lax.ppermute(block, "yh", [(0, 1), (1, 0)])
 
 
 def body(orbitals, cell_matrix, connectivity, surface_nodes, cell_scale, potential):
@@ -275,6 +315,7 @@
     cell_count = connectivity.shape[0]
     inner = cell_count - cell_count // 4
     half = inner // 2
+    side = jnp.stack([lax.axis_index("yh"), lax.axis_index("x")]).astype(jnp.int32)
     older, newest = None, orbitals
     boundary = edge(surface_nodes, newest)
     for degree_step in range(DEGREE):
@@ -282,16 +323,20 @@
         ghosts = behind(boundary, -1)
         first_total = cells(0, half, *cell_args, (newest,))
         shared = cells(inner, cell_count - inner, *cell_args, (newest, ghosts))
-        returned = behind(shared[:, newest.shape[1]:], 1)
-        total = cells(half, inner - half, *cell_args, (newest,), (first_total, shared))
-        result = combine(total, returned, surface_nodes, pot, newest, older, last)
-        older, newest = newest, result[0]
-        boundary = None if last else result[1]
-    field = field_all(newest)
-    rows = lax.dot_general(newest, field, (((1,), (1,)), ((), ())), preferred_element_type=jnp.float32)
+        returned = behind(shared[1], 1)
+        total = cells(half, inner - half, *cell_args, (newest,), (first_total[0], shared[0]))[0]
+        result = combine(side, total, returned, surface_nodes, pot, newest, older, last)
+        older, (newest, boundary) = newest, result
+    keep, send = newest, boundary
+    copies = lax.axis_size("x")
+    pair = arrange(side, keep, turn_over(send), copies)
+    field = swap(pair, "x").reshape(-1, keep.shape[1])
+    rows = lax.dot_general(pair[0], field, (((1,), (1,)), ((), ())), preferred_element_type=jnp.float32)
     node_total = lax.axis_size(DOM) * orbitals.shape[1]
-    start = lax.axis_index(("x", "yh")).astype(jnp.int32)[None]
-    return rotate(start, gram_total(rows), field, orbitals.shape[0], node_total)
+    keep, send = rotate(side, gram_total(rows), field, rows.shape[0], node_total)
+    other = turn_over(send)
+    first = side[0] == 0
+    return jnp.where(first, jnp.concatenate([keep, other], axis=1), jnp.concatenate([other, keep], axis=1))
 
 
 DOM = ("z", "yl", "core")

time: 205 us -> 176 us (0.86)
  waiting for transfers between devices: 57.5 us -> 26.4 us
  blocking collectives: 41.4 us -> 72.2 us
  Pallas kernels: 57.5 us -> 35.4 us
  local copies, waits for them, and re-layouts: 9.59 us -> 5.09 us
  starting transfers between devices: 35.9 us -> 33.8 us
    all_to_all x2 -> x1, waiting for transfers between devices: 46.2 us -> 10.1 us  [swap(): return lax.all_to_all(block, axes, 0, 0, tiled=True)]
    all_to_all x2 -> x4, blocking collectives: 41.4 us -> 72.2 us  [swap(): return lax.all_to_all(block, axes, 0, 0, tiled=True)]
    pallas_call x9, Pallas kernels: 40.4 us -> 24.8 us  [cells(): pl.pallas_call(functools.partial(cells_body, len(adds), first, count, n_b...]
    all_to_all x2 -> x1, starting transfers between devices: 8.46 us -> 3.49 us  [swap(): return lax.all_to_all(block, axes, 0, 0, tiled=True)]
    ppermute x1 -> x2, waiting for transfers between devices: 11.3 us -> 16.2 us  [turn_over(): return lax.ppermute(block, 'yh', [(0, 1), (1, 0)])]
    pallas_call x3, Pallas kernels: 6.83 us -> 3.07 us  [combine(): pl.pallas_call(functools.partial(combine_body, first_step, last_step), ou...]
    ppermute x1 -> x2, starting transfers between devices: 1.91 us -> 4.75 us  [turn_over(): return lax.ppermute(block, 'yh', [(0, 1), (1, 0)])]
    broadcast_in_dim x3 -> x4, local copies, waits for them, and re-layouts: 2.31 us -> 0.09 us  [spread(): jnp.broadcast_to(block[None], (lax.axis_size(axes), *block.shape))]
  transfers between devices with their start and end apart: 9 -> 9, of which waited for: 3 -> 4; matrix products, arithmetic and copies ran while one was open for 0% -> 1% of each run, Pallas kernels for 14% -> 10%
where the time goes in v2:
time: 176 us; the launch traced here: 174 us
  blocking collectives  72.2 us (41%)
  Pallas kernels  35.4 us (20%)
  starting transfers between devices  33.8 us (19%)
  waiting for transfers between devices  26.4 us (15%)
  local copies, waits for them, and re-layouts  5.09 us (3%)
    all_to_all x4, blocking collectives, swap(): return lax.all_to_all(block, axes, 0, 0, tiled=True)  72.2 us
    ppermute x6, starting transfers between devices, behind(): return lax.ppermute(block, DOM, route)  25.5 us
    pallas_call x9, Pallas kernels, cells(): pl.pallas_call(functools.partial(cells_body, len(adds), first, count, n_b...  24.8 us
    ppermute x2, waiting for transfers between devices, turn_over(): return lax.ppermute(block, 'yh', [(0, 1), (1, 0)])  16.2 us
    all_to_all x1, waiting for transfers between devices, swap(): return lax.all_to_all(block, axes, 0, 0, tiled=True)  10.1 us
    pallas_call x1, Pallas kernels, rotate(): pl.pallas_call(functools.partial(rotate_body, node_total), out_shape=[jax...  5.82 us
    ppermute x2, starting transfers between devices, turn_over(): return lax.ppermute(block, 'yh', [(0, 1), (1, 0)])  4.75 us
    unnamed x18, local copies, waits for them, and re-layouts  3.94 us
  transfers between devices with their start and end apart: 9, of which 4 were waited for; matrix products, arithmetic and copies ran while one was open for 1% of the time, Pallas kernels for 10%

profile of v2, /device:TPU:1, one launch (start us, length us, event | category | flops | bytes accessed | tf_op | source)
XLA Modules:
  0.0 174.4 jit_solution(9295582087085449855)
XLA Ops:
  1.8 12.4 %collective-permute-start = (bf16[48,256]{1,0:T(8,128)(2,1)S(1)}, bf16[48,256]{1,0:T(8,128)(2,1)S(1)}, u32[]{:S(2)}, u32[]{:S(2)}) collective-permute-start(bf16[48,256]{1,0:T(8,128)(2,1)S(1)} %edge.1), channel_id=1, source_target_pairs={{8,0},{16,8},{24,16},{32,24},{40,32},{48,40},{56,48},{64,56},{72,6... | collective-permute-start | bytes 73736 | tf_op jit(solution)/shard_map/ppermute | solution.py:287
  15.9 2.9 %cells_0_6.3.refs_3_ = f32[48,2048]{1,0:T(8,128)S(1)} custom-call(f32[16]{0:T(128)S(1)} %copy-done.8, s32[16,512]{1,0:T(8,128)S(1)} %copy-done.6, bf16[512,512]{1,0:T(8,128)(2,1)S(1)} %copy-done.4, bf16[48,2048]{1,0:T(8,128)(2,1)S(1)} %copy-done.1), custom_call_target="tpu_custom_call" | custom-call | flops 5888802816 | bytes 3145728 | tf_op jit(solution)/shard_map/cells_0_6/pallas_call | solution.py:101
  18.9 2.4 %cells_12_4.3 = (f32[48,2048]{1,0:T(8,128)S(1)}, f32[48,256]{1,0:T(8,128)S(1)}) custom-call(f32[16]{0:T(128)S(1)} %copy-done.8, s32[16,512]{1,0:T(8,128)S(1)} %copy-done.6, bf16[512,512]{1,0:T(8,128)(2,1)S(1)} %copy-done.4, bf16[48,2048]{1,0:T(8,128)(2,1)S(1)} %copy-done.1, bf16[48,256]{1,0:T(8,128)(2,1)S(1)} %collective-permute-done.refs_3_), custom_call_target="tpu_custom_call" | custom-call | flops 4378853376 | bytes 3145728 | tf_op jit(solution)/shard_map/cells_12_4/pallas_call | solution.py:101
  23.3 2.9 %cells_6_6.3.total_ref = f32[48,2048]{1,0:T(8,128)S(1)} custom-call(f32[16]{0:T(128)S(1)} %copy-done.8, s32[16,512]{1,0:T(8,128)S(1)} %copy-done.6, bf16[512,512]{1,0:T(8,128)(2,1)S(1)} %copy-done.4, bf16[48,2048]{1,0:T(8,128)(2,1)S(1)} %copy-done.1, f32[48,2048]{1,0:T(8,128)S(1)} %cells_0_6.3.refs_3_, f32[48,2048]{1,0:T(8,128)S(1)} %get-tuple-element.19.refs_4_), custom_call_target="tpu_custom_call" | custom-call | flops 5888802816 | bytes 3145728 | tf_op jit(solution)/shard_map/cells_6_6/pallas_call | solution.py:101
  28.0 2.4 %collective-permute-start.2 = (bf16[48,256]{1,0:T(8,128)(2,1)S(1)}, bf16[48,256]{1,0:T(8,128)(2,1)S(1)}, u32[]{:S(2)}, u32[]{:S(2)}) collective-permute-start(bf16[48,256]{1,0:T(8,128)(2,1)S(1)} %get-tuple-element.22), channel_id=1, source_target_pairs={{8,0},{16,8},{24,16},{32,24},{40,32},{48,40},{56,48},{64,56},{72,6... | collective-permute-start | bytes 73736 | tf_op jit(solution)/shard_map/ppermute | solution.py:287
  30.4 2.9 %cells_0_6.4.refs_3_ = f32[48,2048]{1,0:T(8,128)S(1)} custom-call(f32[16]{0:T(128)S(1)} %copy-done.8, s32[16,512]{1,0:T(8,128)S(1)} %copy-done.6, bf16[512,512]{1,0:T(8,128)(2,1)S(1)} %copy-done.5, bf16[48,2048]{1,0:T(8,128)(2,1)S(1)} %get-tuple-element.21.refs_2_.new_ref.refs_0_), custom_call_target="tpu_custom_call" | custom-call | flops 5888802816 | bytes 3145728 | tf_op jit(solution)/shard_map/cells_0_6/pallas_call | solution.py:101
  33.3 2.4 %cells_12_4.4 = (f32[48,2048]{1,0:T(8,128)S(1)}, f32[48,256]{1,0:T(8,128)S(1)}) custom-call(f32[16]{0:T(128)S(1)} %copy-done.8, s32[16,512]{1,0:T(8,128)S(1)} %copy-done.6, bf16[512,512]{1,0:T(8,128)(2,1)S(1)} %copy-done.5, bf16[48,2048]{1,0:T(8,128)(2,1)S(1)} %get-tuple-element.21.refs_2_.new_ref.refs_0_, bf16[48,256]{1,0:T(8,128)(2,1)S(1)} %collective-permute-done.2.refs_3_), custom_call_target="tpu_custom_call" | custom-call | flops 4378853376 | bytes 3145728 | tf_op jit(solution)/shard_map/cells_12_4/pallas_call | solution.py:101
  35.8 3.2 %collective-permute-start.3 = (f32[48,256]{1,0:T(8,128)S(1)}, f32[48,256]{1,0:T(8,128)S(1)}, u32[]{:S(2)}, u32[]{:S(2)}) collective-permute-start(f32[48,256]{1,0:T(8,128)S(1)} %get-tuple-element.24), channel_id=1, source_target_pairs={{0,8},{8,16},{16,24},{24,32},{32,40},{40,48},{48,56},{56,64},{64,7... | collective-permute-start | bytes 147464 | tf_op jit(solution)/shard_map/ppermute | solution.py:287
  39.0 2.9 %cells_6_6.4.total_ref = f32[48,2048]{1,0:T(8,128)S(1)} custom-call(f32[16]{0:T(128)S(1)} %copy-done.8, s32[16,512]{1,0:T(8,128)S(1)} %copy-done.6, bf16[512,512]{1,0:T(8,128)(2,1)S(1)} %copy-done.5, bf16[48,2048]{1,0:T(8,128)(2,1)S(1)} %get-tuple-element.21.refs_2_.new_ref.refs_0_, f32[48,2048]{1,0:T(8,128)S(1)} %cells_0_6.4.refs_3_, ...), custom_call_target="tpu_custom_call" | custom-call | flops 5888802816 | bytes 3145728 | tf_op jit(solution)/shard_map/cells_6_6/pallas_call | solution.py:101
  43.0 2.1 %collective-permute-start.4 = (bf16[48,256]{1,0:T(8,128)(2,1)S(1)}, bf16[48,256]{1,0:T(8,128)(2,1)S(1)}, u32[]{:S(2)}, u32[]{:S(2)}) collective-permute-start(bf16[48,256]{1,0:T(8,128)(2,1)S(1)} %get-tuple-element.26), channel_id=1, source_target_pairs={{8,0},{16,8},{24,16},{32,24},{40,32},{48,40},{56,48},{64,56},{72,6... | collective-permute-start | bytes 73736 | tf_op jit(solution)/shard_map/ppermute | solution.py:287
  45.1 2.9 %cells_0_6.5.refs_3_ = f32[48,2048]{1,0:T(8,128)S(1)} custom-call(f32[16]{0:T(128)S(1)} %copy-done.8, s32[16,512]{1,0:T(8,128)S(1)} %copy-done.6, bf16[512,512]{1,0:T(8,128)(2,1)S(1)} %copy-done.5, bf16[48,2048]{1,0:T(8,128)(2,1)S(1)} %get-tuple-element.25.refs_2_.new_ref), custom_call_target="tpu_custom_call" | custom-call | flops 5888802816 | bytes 3145728 | tf_op jit(solution)/shard_map/cells_0_6/pallas_call | solution.py:101
  48.1 2.4 %cells_12_4.5 = (f32[48,2048]{1,0:T(8,128)S(1)}, f32[48,256]{1,0:T(8,128)S(1)}) custom-call(f32[16]{0:T(128)S(1)} %copy-done.8, s32[16,512]{1,0:T(8,128)S(1)} %copy-done.6, bf16[512,512]{1,0:T(8,128)(2,1)S(1)} %copy-done.5, bf16[48,2048]{1,0:T(8,128)(2,1)S(1)} %get-tuple-element.25.refs_2_.new_ref, bf16[48,256]{1,0:T(8,128)(2,1)S(1)} %collective-permute-done.4.refs_3_), custom_call_target="tpu_custom_call" | custom-call | flops 4378853376 | bytes 3145728 | tf_op jit(solution)/shard_map/cells_12_4/pallas_call | solution.py:101
  50.6 3.5 %collective-permute-start.5 = (f32[48,256]{1,0:T(8,128)S(1)}, f32[48,256]{1,0:T(8,128)S(1)}, u32[]{:S(2)}, u32[]{:S(2)}) collective-permute-start(f32[48,256]{1,0:T(8,128)S(1)} %get-tuple-element.28), channel_id=1, source_target_pairs={{0,8},{8,16},{16,24},{24,32},{32,40},{40,48},{48,56},{56,64},{64,7... | collective-permute-start | bytes 147464 | tf_op jit(solution)/shard_map/ppermute | solution.py:287
  54.1 2.9 %cells_6_6.5.total_ref = f32[48,2048]{1,0:T(8,128)S(1)} custom-call(f32[16]{0:T(128)S(1)} %copy-done.8, s32[16,512]{1,0:T(8,128)S(1)} %copy-done.6, bf16[512,512]{1,0:T(8,128)(2,1)S(1)} %copy-done.5, bf16[48,2048]{1,0:T(8,128)(2,1)S(1)} %get-tuple-element.25.refs_2_.new_ref, f32[48,2048]{1,0:T(8,128)S(1)} %cells_0_6.5.refs_3_, ...), custom_call_target="tpu_custom_call" | custom-call | flops 5888802816 | bytes 3145728 | tf_op jit(solution)/shard_map/cells_6_6/pallas_call | solution.py:101
  59.9 9.7 %collective-permute-done.6.other_ref = bf16[48,1024]{1,0:T(8,128)(2,1)S(1)} collective-permute-done((bf16[48,1024]{1,0:T(8,128)(2,1)S(1)}, bf16[48,1024]{1,0:T(8,128)(2,1)S(1)}, u32[]{:S(2)}, u32[]{:S(2)}) %collective-permute-start.6) | collective-permute-done | bytes 98336 | tf_op jit(solution)/shard_map/ppermute | solution.py:309
  71.0 3.5 %all-to-all-start = ((bf16[4,96,1024]{2,1,0:T(8,128)(2,1)}), bf16[4,96,1024]{2,1,0:T(8,128)(2,1)S(1)}, u32[]{:S(2)}, u32[]{:S(2)}) async-start(bf16[4,96,1024]{2,1,0:T(8,128)(2,1)} %arrange.1), calls=%async_computation | async-start | bytes 1572864 | tf_op jit(solution)/shard_map/all_to_all | solution.py:291
  75.5 10.1 %all-to-all-done = bf16[4,96,1024]{2,1,0:T(8,128)(2,1)S(1)} async-done(((bf16[4,96,1024]{2,1,0:T(8,128)(2,1)}), bf16[4,96,1024]{2,1,0:T(8,128)(2,1)S(1)}, u32[]{:S(2)}, u32[]{:S(2)}) %all-to-all-start) | async-done | bytes 786464 | tf_op jit(solution)/shard_map/all_to_all | solution.py:291
  86.0 17.0 %all_to_all.25 = f32[16,6,384]{2,1,0:T(8,128)S(1)} all-to-all(f32[16,6,384]{2,1,0:T(8,128)S(1)} %copy.12), channel_id=1, replica_groups=mesh['z'=12,'yl'=4,'core'=2,'yh'=2,'x'=4] {'yl','core','yh'}, dimensions={0} | all-to-all | bytes 294912 | tf_op jit(solution)/shard_map/all_to_all | solution.py:291
  103.1 28.2 %all_to_all.26 = f32[12,6,384]{2,1,0:T(8,128)S(1)} all-to-all(f32[12,6,384]{2,1,0:T(8,128)S(1)} %broadcast_in_dim.11), channel_id=1, replica_groups=mesh['z'=12,'yl'=4,'core'=2,'yh'=2,'x'=4] {'z'}, dimensions={0} | all-to-all | bytes 221184 | tf_op jit(solution)/shard_map/all_to_all | solution.py:291
  131.3 15.3 %all_to_all.27 = f32[16,6,384]{2,1,0:T(8,128)S(1)} all-to-all(f32[16,6,384]{2,1,0:T(8,128)S(1)} %broadcast_in_dim.24), channel_id=1, replica_groups=mesh['z'=12,'yl'=4,'core'=2,'yh'=2,'x'=4] {'yl','core','yh'}, dimensions={0} | all-to-all | bytes 294912 | tf_op jit(solution)/shard_map/all_to_all | solution.py:291
  146.7 11.8 %all_to_all.28 = f32[4,96,384]{2,1,0:T(8,128)S(1)} all-to-all(f32[4,96,384]{2,1,0:T(8,128)S(1)} %broadcast_in_dim.26), channel_id=1, replica_groups=mesh['z'=12,'yl'=4,'core'=2,'yh'=2,'x'=4] {'x'}, dimensions={0} | all-to-all | bytes 1179648 | tf_op jit(solution)/shard_map/all_to_all | solution.py:291
  158.5 5.8 %rotate.1 = (bf16[48,1024]{1,0:T(8,128)(2,1)S(1)}, bf16[48,1024]{1,0:T(8,128)(2,1)S(1)}) custom-call(s32[2]{0:T(128)S(1)} %pad_add_fusion.side_ref, f32[384,384]{1,0:T(8,128)S(1)} %bitcast.10, bf16[384,1024]{1,0:T(8,128)(2,1)S(1)} %bitcast.9), custom_call_target="tpu_custom_call" | custom-call | tf_op jit(solution)/shard_map/rotate/pallas_call | solution.py:273
  164.3 2.8 %collective-permute-start.7 = (bf16[48,1024]{1,0:T(8,128)(2,1)S(1)}, bf16[48,1024]{1,0:T(8,128)(2,1)S(1)}, u32[]{:S(2)}, u32[]{:S(2)}) collective-permute-start(bf16[48,1024]{1,0:T(8,128)(2,1)S(1)} %get-tuple-element.32), channel_id=1, source_target_pairs={{0,4},{4,0},{1,5},{5,1},{2,6},{6,2},{3,7},{7,3},{8,12},{12,8},{9,1... | collective-permute-start | bytes 294920 | tf_op jit(solution)/shard_map/ppermute | solution.py:309
  167.1 6.5 %collective-permute-done.7 = bf16[48,1024]{1,0:T(8,128)(2,1)S(1)} collective-permute-done((bf16[48,1024]{1,0:T(8,128)(2,1)S(1)}, bf16[48,1024]{1,0:T(8,128)(2,1)S(1)}, u32[]{:S(2)}, u32[]{:S(2)}) %collective-permute-start.7) | collective-permute-done | bytes 98336 | tf_op jit(solution)/shard_map/ppermute | solution.py:309
  (43 shorter events, 15.1 us)
Async XLA Ops:
  0.0 0.9 copy-start
  0.9 0.7 copy-start.2
  1.6 12.6 %copy-start.1 = (bf16[48,2048]{1,0:T(8,128)(2,1)S(1)}, bf16[48,2048]{1,0:T(8,128)(2,1)}, u32[]{:S(2)}) copy-start(bf16[48,2048]{1,0:T(8,128)(2,1)} %refs_0_.16) | copy-start | bytes 589828
  1.6 12.6 %copy-start.6 = (s32[16,512]{1,0:T(8,128)S(1)}, s32[16,512]{1,0:T(8,128)}, u32[]{:S(2)}) copy-start(s32[16,512]{1,0:T(8,128)} %refs_0_.19) | copy-start | bytes 98308
  1.8 17.1 %collective-permute-start = (bf16[48,256]{1,0:T(8,128)(2,1)S(1)}, bf16[48,256]{1,0:T(8,128)(2,1)S(1)}, u32[]{:S(2)}, u32[]{:S(2)}) collective-permute-start(bf16[48,256]{1,0:T(8,128)(2,1)S(1)} %edge.1), channel_id=1, source_target_pairs={{8,0},{16,8},{24,16},{32,24},{40,32},{48,40},{56,48},{64,56},{72,6... | collective-permute-start | bytes 73736 | tf_op jit(solution)/shard_map/ppermute | solution.py:287
  14.2 0.7 copy-start.8
  14.9 1.0 copy-start.4
  21.4 4.9 %collective-permute-start.1 = (f32[48,256]{1,0:T(8,128)S(1)}, f32[48,256]{1,0:T(8,128)S(1)}, u32[]{:S(2)}, u32[]{:S(2)}) collective-permute-start(f32[48,256]{1,0:T(8,128)S(1)} %get-tuple-element.20), channel_id=1, source_target_pairs={{0,8},{8,16},{16,24},{24,32},{32,40},{40,48},{48,56},{56,64},{64,7... | collective-permute-start | bytes 147464 | tf_op jit(solution)/shard_map/ppermute | solution.py:287
  23.3 3.0 %copy-start.7 = (f32[2048]{0:T(1024)S(1)}, f32[2048]{0:T(1024)}, u32[]{:S(2)}) copy-start(f32[2048]{0:T(1024)} %param.11) | copy-start | bytes 24580
  26.2 0.7 copy-start.3
  26.2 4.2 %copy-start.5 = (bf16[512,512]{1,0:T(8,128)(2,1)S(1)}, bf16[512,512]{1,0:T(8,128)(2,1)}, u32[]{:S(2)}) copy-start(bf16[512,512]{1,0:T(8,128)(2,1)} %refs_1_.17) | copy-start | bytes 1572868
  28.0 5.3 %collective-permute-start.2 = (bf16[48,256]{1,0:T(8,128)(2,1)S(1)}, bf16[48,256]{1,0:T(8,128)(2,1)S(1)}, u32[]{:S(2)}, u32[]{:S(2)}) collective-permute-start(bf16[48,256]{1,0:T(8,128)(2,1)S(1)} %get-tuple-element.22), channel_id=1, source_target_pairs={{8,0},{16,8},{24,16},{32,24},{40,32},{48,40},{56,48},{64,56},{72,6... | collective-permute-start | bytes 73736 | tf_op jit(solution)/shard_map/ppermute | solution.py:287
  35.8 6.1 %collective-permute-start.3 = (f32[48,256]{1,0:T(8,128)S(1)}, f32[48,256]{1,0:T(8,128)S(1)}, u32[]{:S(2)}, u32[]{:S(2)}) collective-permute-start(f32[48,256]{1,0:T(8,128)S(1)} %get-tuple-element.24), channel_id=1, source_target_pairs={{0,8},{8,16},{16,24},{24,32},{32,40},{40,48},{48,56},{56,64},{64,7... | collective-permute-start | bytes 147464 | tf_op jit(solution)/shard_map/ppermute | solution.py:287
  43.0 5.1 %collective-permute-start.4 = (bf16[48,256]{1,0:T(8,128)(2,1)S(1)}, bf16[48,256]{1,0:T(8,128)(2,1)S(1)}, u32[]{:S(2)}, u32[]{:S(2)}) collective-permute-start(bf16[48,256]{1,0:T(8,128)(2,1)S(1)} %get-tuple-element.26), channel_id=1, source_target_pairs={{8,0},{16,8},{24,16},{32,24},{40,32},{48,40},{56,48},{64,56},{72,6... | collective-permute-start | bytes 73736 | tf_op jit(solution)/shard_map/ppermute | solution.py:287
  50.6 6.5 %collective-permute-start.5 = (f32[48,256]{1,0:T(8,128)S(1)}, f32[48,256]{1,0:T(8,128)S(1)}, u32[]{:S(2)}, u32[]{:S(2)}) collective-permute-start(f32[48,256]{1,0:T(8,128)S(1)} %get-tuple-element.28), channel_id=1, source_target_pairs={{0,8},{8,16},{16,24},{24,32},{32,40},{40,48},{48,56},{56,64},{64,7... | collective-permute-start | bytes 147464 | tf_op jit(solution)/shard_map/ppermute | solution.py:287
  58.0 11.6 %collective-permute-start.6 = (bf16[48,1024]{1,0:T(8,128)(2,1)S(1)}, bf16[48,1024]{1,0:T(8,128)(2,1)S(1)}, u32[]{:S(2)}, u32[]{:S(2)}) collective-permute-start(bf16[48,1024]{1,0:T(8,128)(2,1)S(1)} %get-tuple-element.30), channel_id=1, source_target_pairs={{0,4},{4,0},{1,5},{5,1},{2,6},{6,2},{3,7},{7,3},{8,12},{12,8},{9,1... | collective-permute-start | bytes 294920 | tf_op jit(solution)/shard_map/ppermute | solution.py:309
  71.0 14.6 %all-to-all-start = ((bf16[4,96,1024]{2,1,0:T(8,128)(2,1)}), bf16[4,96,1024]{2,1,0:T(8,128)(2,1)S(1)}, u32[]{:S(2)}, u32[]{:S(2)}) async-start(bf16[4,96,1024]{2,1,0:T(8,128)(2,1)} %arrange.1), calls=%async_computation | async-start | bytes 1572864 | tf_op jit(solution)/shard_map/all_to_all | solution.py:291
  164.3 9.4 %collective-permute-start.7 = (bf16[48,1024]{1,0:T(8,128)(2,1)S(1)}, bf16[48,1024]{1,0:T(8,128)(2,1)S(1)}, u32[]{:S(2)}, u32[]{:S(2)}) collective-permute-start(bf16[48,1024]{1,0:T(8,128)(2,1)S(1)} %get-tuple-element.32), channel_id=1, source_target_pairs={{0,4},{4,0},{1,5},{5,1},{2,6},{6,2},{3,7},{7,3},{8,12},{12,8},{9,1... | collective-permute-start | bytes 294920 | tf_op jit(solution)/shard_map/ppermute | solution.py:309

commit v3 on v2

--- a/solution.py
+++ b/solution.py
@@ -113,7 +113,7 @@
     )(scale, conn, matrix, *srcs, *adds)
 
 
-def combine_body(first_step, last_step, side_ref, total_ref, back_ref, surf_ref, pot_ref, new_ref, *refs):
+def combine_body(first_step, last_step, total_ref, back_ref, surf_ref, pot_ref, new_ref, *refs):
     refs = list(refs)
     old_ref = None if first_step else refs.pop(0)
     out_ref = refs.pop(0)
@@ -145,13 +145,11 @@
             out_ref[:, span] = fresh
         fresh_blocks.append(fresh)
     if last_step:
-        first = side_ref[0] == 0
         middle = n_blocks // 2
-        for b in range(middle):
-            span = slice(b * LOW, (b + 1) * LOW)
-            early, late = fresh_blocks[b], fresh_blocks[middle + b]
-            out_ref[:, span] = jnp.where(first, early, late)
-            refs[0][:, span] = jnp.where(first, late, early)
+        for part in range(2):
+            block = jnp.concatenate(fresh_blocks[part * middle : (part + 1) * middle], axis=1)
+            for copy in range(out_ref.shape[1]):
+                out_ref[part, copy] = block
     else:
         refs[0][...] = edge_values(row, hot, fresh_blocks)
 
@@ -163,26 +161,26 @@
     return pick_block(tile_rows(row >> 8, states), blocks).astype(jnp.bfloat16)
 
 
-def combine(side, total, back, surf, pot, newest, older, last_step):
+def combine(total, back, surf, pot, newest, older, copies):
+    last_step = copies > 0
     first_step = older is None
     states, nodes = newest.shape
     edge = surf.shape[1]
     vmem = pl.BlockSpec(memory_space=pltpu.VMEM)
     olds = () if first_step else (older,)
     if last_step:
-        outs = [jax.ShapeDtypeStruct((states, nodes // 2), jnp.bfloat16)] * 2
+        outs = [jax.ShapeDtypeStruct((2, copies, states, nodes // 2), jnp.bfloat16)]
     else:
         outs = [jax.ShapeDtypeStruct((states, n), jnp.bfloat16) for n in (nodes, edge)]
-    smem = pl.BlockSpec(memory_space=pltpu.SMEM)
     return pl.pallas_call(
         functools.partial(combine_body, first_step, last_step),
         out_shape=outs,
-        in_specs=[smem] + [vmem] * (5 + len(olds)),
+        in_specs=[vmem] * (5 + len(olds)),
         out_specs=[vmem] * len(outs),
         cost_estimate=pl.CostEstimate(flops=1 << 28, bytes_accessed=1 << 20, transcendentals=0),
         compiler_params=pltpu.CompilerParams(vmem_limit_bytes=VMEM_LIMIT),
         name="combine",
-    )(side, total, back, surf, pot, newest, *olds)
+    )(total, back, surf, pot, newest, *olds)
 
 
 def edge_body(surf_ref, new_ref, out_ref):
@@ -216,34 +214,39 @@
     return dot(jnp.concatenate([ah, al, ah], axis=1), jnp.concatenate([bh, bh, bl], axis=0))
 
 
-def arrange_body(side_ref, keep_ref, other_ref, out_ref):
-    first = side_ref[0] == 0
-    states = keep_ref.shape[0]
-    keep, other = keep_ref[...], other_ref[...]
-    early, late = jnp.where(first, keep, other), jnp.where(first, other, keep)
+def own_rows(side_ref, ref, states):
+    other = ref.shape[0] // 2
+    start = pl.multiple_of(side_ref[1] * states, 16)
+    return jnp.concatenate([ref[pl.ds(start, states), :], ref[pl.ds(start + other, states), :]], axis=0)
+
+
+def gram_body(states, side_ref, field_ref, out_ref):
+    rows = lax.dot_general(
+        own_rows(side_ref, field_ref, states), field_ref[...], (((1,), (1,)), ((), ())),
+        preferred_element_type=jnp.float32)
+    depth = out_ref.shape[1]
     for i in range(out_ref.shape[0]):
-        out_ref[i, :states] = early
-        out_ref[i, states:] = late
-
-
-def arrange(side, keep, other, copies):
+        out_ref[i] = rows[i * depth : (i + 1) * depth]
+
+
+def gram_rows(side, field, states, pieces):
     smem = pl.BlockSpec(memory_space=pltpu.SMEM)
     vmem = pl.BlockSpec(memory_space=pltpu.VMEM)
-    states, nodes = keep.shape
-    return pl.pallas_call(
-        arrange_body,
-        out_shape=jax.ShapeDtypeStruct((copies, 2 * states, nodes), jnp.bfloat16),
-        in_specs=[smem, vmem, vmem],
+    return pl.pallas_call(
+        functools.partial(gram_body, states),
+        out_shape=jax.ShapeDtypeStruct((pieces, 2 * states // pieces, field.shape[0]), jnp.float32),
+        in_specs=[smem, vmem],
         out_specs=vmem,
         compiler_params=pltpu.CompilerParams(vmem_limit_bytes=VMEM_LIMIT),
-        name="arrange",
-    )(side, keep, other)
-
-
-def rotate_body(node_total, side_ref, gram_ref, field_ref, keep_ref, send_ref, high_ref, turned_ref):
-    gram = gram_ref[...]
-    rows = turned_ref.shape[0]
-    half = rows // 2
+        name="gram",
+    )(side, field)
+
+
+def rotate_body(node_total, side_ref, here_ref, there_ref, field_ref, keep_ref, send_ref, high_ref, turned_ref):
+    first = side_ref[2] == 0
+    here, there = here_ref[...], there_ref[...]
+    gram = jnp.concatenate([jnp.where(first, here, there), jnp.where(first, there, here)], axis=0)
+    half = keep_ref.shape[0]
     scale_sum = jnp.sqrt(jnp.sum(gram * gram, keepdims=True)) + epsilon
     eye = (
         lax.broadcasted_iota(jnp.int32, gram.shape, 0) == lax.broadcasted_iota(jnp.int32, gram.shape, 1)
@@ -257,8 +260,7 @@
             inverse = product(inverse, factor)
         factor = 1.5 * eye - 0.5 * product(growing, inverse)
     high_ref[...] = inverse
-    mine = high_ref[pl.ds(pl.multiple_of(side_ref[1] * rows, 32), rows), :]
-    mine = product(mine, factor)
+    mine = product(own_rows(side_ref, high_ref, half), factor)
     turn = (mine * jnp.sqrt(node_total / scale_sum)).astype(jnp.bfloat16)
     turned_ref[...] = jnp.dot(turn, field_ref[...], preferred_element_type=jnp.float32).astype(jnp.bfloat16)
     side = side_ref[0]
@@ -266,19 +268,19 @@
     send_ref[...] = turned_ref[pl.ds(pl.multiple_of((1 - side) * half, 16), half), :]
 
 
-def rotate(side, gram, field, rows, node_total):
+def rotate(side, here, there, field, states, node_total):
     smem = pl.BlockSpec(memory_space=pltpu.SMEM)
     vmem = pl.BlockSpec(memory_space=pltpu.VMEM)
-    nodes = field.shape[1]
+    total, nodes = field.shape
     return pl.pallas_call(
         functools.partial(rotate_body, node_total),
-        out_shape=[jax.ShapeDtypeStruct((rows // 2, nodes), jnp.bfloat16)] * 2,
-        in_specs=[smem, vmem, vmem],
+        out_shape=[jax.ShapeDtypeStruct((states, nodes), jnp.bfloat16)] * 2,
+        in_specs=[smem, vmem, vmem, vmem],
         out_specs=[vmem] * 2,
-        scratch_shapes=[pltpu.VMEM(gram.shape, jnp.float32), pltpu.VMEM((rows, nodes), jnp.bfloat16)],
+        scratch_shapes=[pltpu.VMEM((total, total), jnp.float32), pltpu.VMEM((2 * states, nodes), jnp.bfloat16)],
         compiler_params=pltpu.CompilerParams(vmem_limit_bytes=VMEM_LIMIT),
         name="rotate",
-    )(side, gram, field)
+    )(side, here, there, field)
 
 
 def behind(block, distance):
@@ -295,18 +297,15 @@
     return swap(jnp.broadcast_to(block[None], (lax.axis_size(axes), *block.shape)), axes)
 
 
-def gram_total(rows):
-    states, columns = rows.shape
-    near = ("yl", "core", "yh")
-    count = lax.axis_size(near)
-    part = jnp.sum(swap(rows.reshape(count, states // count, columns), near), axis=0)
+def gram_halves(rows):
+    part = jnp.sum(swap(rows, ("core", "yl", "yh")), axis=0)
     part = jnp.sum(spread(part, "z"), axis=0)
-    block = spread(part, near).reshape(states, columns)
-    return spread(block, "x").reshape(-1, columns)
-
-
-def turn_over(block):
-    return lax.ppermute(block, "yh", [(0, 1), (1, 0)])
+    here = spread(part, ("x", "yl", "yh")).reshape(-1, rows.shape[-1])
+    return here, turn_over(here, "core")
+
+
+def turn_over(block, axis):
+    return lax.ppermute(block, axis, [(0, 1), (1, 0)])
 
 
 def body(orbitals, cell_matrix, connectivity, surface_nodes, cell_scale, potential):
@@ -315,26 +314,26 @@
     cell_count = connectivity.shape[0]
     inner = cell_count - cell_count // 4
     half = inner // 2
-    side = jnp.stack([lax.axis_index("yh"), lax.axis_index("x")]).astype(jnp.int32)
+    side = jnp.stack([lax.axis_index(name) for name in ("yh", "x", "core")]).astype(jnp.int32)
     older, newest = None, orbitals
     boundary = edge(surface_nodes, newest)
     for degree_step in range(DEGREE):
-        last = degree_step == DEGREE - 1
         ghosts = behind(boundary, -1)
         first_total = cells(0, half, *cell_args, (newest,))
         shared = cells(inner, cell_count - inner, *cell_args, (newest, ghosts))
         returned = behind(shared[1], 1)
         total = cells(half, inner - half, *cell_args, (newest,), (first_total[0], shared[0]))[0]
-        result = combine(side, total, returned, surface_nodes, pot, newest, older, last)
-        older, (newest, boundary) = newest, result
-    keep, send = newest, boundary
-    copies = lax.axis_size("x")
-    pair = arrange(side, keep, turn_over(send), copies)
-    field = swap(pair, "x").reshape(-1, keep.shape[1])
-    rows = lax.dot_general(pair[0], field, (((1,), (1,)), ((), ())), preferred_element_type=jnp.float32)
+        copies = lax.axis_size("x") if degree_step == DEGREE - 1 else 0
+        result = combine(total, returned, surface_nodes, pot, newest, older, copies)
+        older, newest = newest, result[0]
+        boundary = result[-1]
+    states, field = orbitals.shape[0], newest
+    field = swap(field.reshape(-1, *field.shape[2:]), ST).reshape(-1, field.shape[3])
+    pieces = lax.axis_size(("core", "yl", "yh"))
+    here, there = gram_halves(gram_rows(side, field, states, pieces))
     node_total = lax.axis_size(DOM) * orbitals.shape[1]
-    keep, send = rotate(side, gram_total(rows), field, rows.shape[0], node_total)
-    other = turn_over(send)
+    keep, send = rotate(side, here, there, field, states, node_total)
+    other = turn_over(send, "yh")
     first = side[0] == 0
     return jnp.where(first, jnp.concatenate([keep, other], axis=1), jnp.concatenate([other, keep], axis=1))
 

time: 176 us -> 170 us (0.966)
  blocking collectives: 72.2 us -> 57.8 us
  waiting for transfers between devices: 26.4 us -> 32.5 us
  starting transfers between devices: 33.8 us -> 39.4 us
    all_to_all x4 -> x3, blocking collectives: 72.2 us -> 57.8 us  [swap(): return lax.all_to_all(block, axes, 0, 0, tiled=True)]
    all_to_all x1, waiting for transfers between devices: 10.1 us -> 22.6 us  [swap(): return lax.all_to_all(block, axes, 0, 0, tiled=True)]
    ppermute x2, waiting for transfers between devices: 16.2 us -> 9.76 us  [turn_over(): return lax.ppermute(block, axis, [(0, 1), (1, 0)])]
    ppermute x2, starting transfers between devices: 4.75 us -> 10.3 us  [turn_over(): return lax.ppermute(block, axis, [(0, 1), (1, 0)])]
  transfers between devices with their start and end apart: 9 -> 9, of which waited for: 4 -> 4; matrix products, arithmetic and copies ran while one was open for 1% -> 0% of each run, Pallas kernels for 10% -> 10%
where the time goes in v3:
time: 170 us; the launch traced here: 169 us
  blocking collectives  57.8 us (34%)
  starting transfers between devices  39.4 us (23%)
  Pallas kernels  34.1 us (20%)
  waiting for transfers between devices  32.5 us (19%)
  local copies, waits for them, and re-layouts  4.15 us (2%)
    all_to_all x3, blocking collectives, swap(): return lax.all_to_all(block, axes, 0, 0, tiled=True)  57.8 us
    ppermute x6, starting transfers between devices, behind(): return lax.ppermute(block, DOM, route)  25.5 us
    pallas_call x9, Pallas kernels, cells(): pl.pallas_call(functools.partial(cells_body, len(adds), first, count, n_b...  24.7 us
    all_to_all x1, waiting for transfers between devices, swap(): return lax.all_to_all(block, axes, 0, 0, tiled=True)  22.6 us
    ppermute x2, starting transfers between devices, turn_over(): return lax.ppermute(block, axis, [(0, 1), (1, 0)])  10.3 us
    ppermute x2, waiting for transfers between devices, turn_over(): return lax.ppermute(block, axis, [(0, 1), (1, 0)])  9.76 us
    pallas_call x1, Pallas kernels, rotate(): pl.pallas_call(functools.partial(rotate_body, node_total), out_shape=[jax...  5.87 us
    unnamed x18, local copies, waits for them, and re-layouts  4.06 us
  transfers between devices with their start and end apart: 9, of which 4 were waited for; matrix products, arithmetic and copies ran while one was open for 0% of the time, Pallas kernels for 10%

profile of v3, /device:TPU:1, one launch (start us, length us, event | category | flops | bytes accessed | tf_op | source)
XLA Modules:
  0.0 169.0 jit_solution(304251005596620106)
XLA Ops:
  1.8 12.4 %collective-permute-start = (bf16[48,256]{1,0:T(8,128)(2,1)S(1)}, bf16[48,256]{1,0:T(8,128)(2,1)S(1)}, u32[]{:S(2)}, u32[]{:S(2)}) collective-permute-start(bf16[48,256]{1,0:T(8,128)(2,1)S(1)} %edge.1), channel_id=1, source_target_pairs={{8,0},{16,8},{24,16},{32,24},{40,32},{48,40},{56,48},{64,56},{72,6... | collective-permute-start | bytes 73736 | tf_op jit(solution)/shard_map/ppermute | solution.py:289
  16.0 2.9 %cells_0_6.3.refs_3_ = f32[48,2048]{1,0:T(8,128)S(1)} custom-call(f32[16]{0:T(128)S(1)} %copy-done.8, s32[16,512]{1,0:T(8,128)S(1)} %copy-done.7, bf16[512,512]{1,0:T(8,128)(2,1)S(1)} %copy-done.5, bf16[48,2048]{1,0:T(8,128)(2,1)S(1)} %copy-done.1), custom_call_target="tpu_custom_call" | custom-call | flops 5888802816 | bytes 3145728 | tf_op jit(solution)/shard_map/cells_0_6/pallas_call | solution.py:101
  19.0 2.4 %cells_12_4.3 = (f32[48,2048]{1,0:T(8,128)S(1)}, f32[48,256]{1,0:T(8,128)S(1)}) custom-call(f32[16]{0:T(128)S(1)} %copy-done.8, s32[16,512]{1,0:T(8,128)S(1)} %copy-done.7, bf16[512,512]{1,0:T(8,128)(2,1)S(1)} %copy-done.5, bf16[48,2048]{1,0:T(8,128)(2,1)S(1)} %copy-done.1, bf16[48,256]{1,0:T(8,128)(2,1)S(1)} %collective-permute-done.refs_3_), custom_call_target="tpu_custom_call" | custom-call | flops 4378853376 | bytes 3145728 | tf_op jit(solution)/shard_map/cells_12_4/pallas_call | solution.py:101
  21.4 1.9 %collective-permute-start.1 = (f32[48,256]{1,0:T(8,128)S(1)}, f32[48,256]{1,0:T(8,128)S(1)}, u32[]{:S(2)}, u32[]{:S(2)}) collective-permute-start(f32[48,256]{1,0:T(8,128)S(1)} %get-tuple-element.18), channel_id=1, source_target_pairs={{0,8},{8,16},{16,24},{24,32},{32,40},{40,48},{48,56},{56,64},{64,7... | collective-permute-start | bytes 147464 | tf_op jit(solution)/shard_map/ppermute | solution.py:289
  23.4 2.9 %cells_6_6.3.total_ref = f32[48,2048]{1,0:T(8,128)S(1)} custom-call(f32[16]{0:T(128)S(1)} %copy-done.8, s32[16,512]{1,0:T(8,128)S(1)} %copy-done.7, bf16[512,512]{1,0:T(8,128)(2,1)S(1)} %copy-done.5, bf16[48,2048]{1,0:T(8,128)(2,1)S(1)} %copy-done.1, f32[48,2048]{1,0:T(8,128)S(1)} %cells_0_6.3.refs_3_, f32[48,2048]{1,0:T(8,128)S(1)} %get-tuple-element.17.refs_4_), custom_call_target="tpu_custom_call" | custom-call | flops 5888802816 | bytes 3145728 | tf_op jit(solution)/shard_map/cells_6_6/pallas_call | solution.py:101
  27.5 2.4 %collective-permute-start.2 = (bf16[48,256]{1,0:T(8,128)(2,1)S(1)}, bf16[48,256]{1,0:T(8,128)(2,1)S(1)}, u32[]{:S(2)}, u32[]{:S(2)}) collective-permute-start(bf16[48,256]{1,0:T(8,128)(2,1)S(1)} %get-tuple-element.20), channel_id=1, source_target_pairs={{8,0},{16,8},{24,16},{32,24},{40,32},{48,40},{56,48},{64,56},{72,6... | collective-permute-start | bytes 73736 | tf_op jit(solution)/shard_map/ppermute | solution.py:289
  29.9 2.9 %cells_0_6.4.refs_3_ = f32[48,2048]{1,0:T(8,128)S(1)} custom-call(f32[16]{0:T(128)S(1)} %copy-done.8, s32[16,512]{1,0:T(8,128)S(1)} %copy-done.7, bf16[512,512]{1,0:T(8,128)(2,1)S(1)} %copy-done.6, bf16[48,2048]{1,0:T(8,128)(2,1)S(1)} %get-tuple-element.19.refs_2_.new_ref.refs_0_), custom_call_target="tpu_custom_call" | custom-call | flops 5888802816 | bytes 3145728 | tf_op jit(solution)/shard_map/cells_0_6/pallas_call | solution.py:101
  32.9 2.4 %cells_12_4.4 = (f32[48,2048]{1,0:T(8,128)S(1)}, f32[48,256]{1,0:T(8,128)S(1)}) custom-call(f32[16]{0:T(128)S(1)} %copy-done.8, s32[16,512]{1,0:T(8,128)S(1)} %copy-done.7, bf16[512,512]{1,0:T(8,128)(2,1)S(1)} %copy-done.6, bf16[48,2048]{1,0:T(8,128)(2,1)S(1)} %get-tuple-element.19.refs_2_.new_ref.refs_0_, bf16[48,256]{1,0:T(8,128)(2,1)S(1)} %collective-permute-done.2.refs_3_), custom_call_target="tpu_custom_call" | custom-call | flops 4378853376 | bytes 3145728 | tf_op jit(solution)/shard_map/cells_12_4/pallas_call | solution.py:101
  35.3 3.2 %collective-permute-start.3 = (f32[48,256]{1,0:T(8,128)S(1)}, f32[48,256]{1,0:T(8,128)S(1)}, u32[]{:S(2)}, u32[]{:S(2)}) collective-permute-start(f32[48,256]{1,0:T(8,128)S(1)} %get-tuple-element.22), channel_id=1, source_target_pairs={{0,8},{8,16},{16,24},{24,32},{32,40},{40,48},{48,56},{56,64},{64,7... | collective-permute-start | bytes 147464 | tf_op jit(solution)/shard_map/ppermute | solution.py:289
  38.5 2.9 %cells_6_6.4.total_ref = f32[48,2048]{1,0:T(8,128)S(1)} custom-call(f32[16]{0:T(128)S(1)} %copy-done.8, s32[16,512]{1,0:T(8,128)S(1)} %copy-done.7, bf16[512,512]{1,0:T(8,128)(2,1)S(1)} %copy-done.6, bf16[48,2048]{1,0:T(8,128)(2,1)S(1)} %get-tuple-element.19.refs_2_.new_ref.refs_0_, f32[48,2048]{1,0:T(8,128)S(1)} %cells_0_6.4.refs_3_, ...), custom_call_target="tpu_custom_call" | custom-call | flops 5888802816 | bytes 3145728 | tf_op jit(solution)/shard_map/cells_6_6/pallas_call | solution.py:101
  42.0 2.1 %collective-permute-start.4 = (bf16[48,256]{1,0:T(8,128)(2,1)S(1)}, bf16[48,256]{1,0:T(8,128)(2,1)S(1)}, u32[]{:S(2)}, u32[]{:S(2)}) collective-permute-start(bf16[48,256]{1,0:T(8,128)(2,1)S(1)} %get-tuple-element.24), channel_id=1, source_target_pairs={{8,0},{16,8},{24,16},{32,24},{40,32},{48,40},{56,48},{64,56},{72,6... | collective-permute-start | bytes 73736 | tf_op jit(solution)/shard_map/ppermute | solution.py:289
  44.1 2.9 %cells_0_6.5.refs_3_ = f32[48,2048]{1,0:T(8,128)S(1)} custom-call(f32[16]{0:T(128)S(1)} %copy-done.8, s32[16,512]{1,0:T(8,128)S(1)} %copy-done.7, bf16[512,512]{1,0:T(8,128)(2,1)S(1)} %copy-done.6, bf16[48,2048]{1,0:T(8,128)(2,1)S(1)} %get-tuple-element.23.refs_2_.new_ref), custom_call_target="tpu_custom_call" | custom-call | flops 5888802816 | bytes 3145728 | tf_op jit(solution)/shard_map/cells_0_6/pallas_call | solution.py:101
  47.1 2.4 %cells_12_4.5 = (f32[48,2048]{1,0:T(8,128)S(1)}, f32[48,256]{1,0:T(8,128)S(1)}) custom-call(f32[16]{0:T(128)S(1)} %copy-done.8, s32[16,512]{1,0:T(8,128)S(1)} %copy-done.7, bf16[512,512]{1,0:T(8,128)(2,1)S(1)} %copy-done.6, bf16[48,2048]{1,0:T(8,128)(2,1)S(1)} %get-tuple-element.23.refs_2_.new_ref, bf16[48,256]{1,0:T(8,128)(2,1)S(1)} %collective-permute-done.4.refs_3_), custom_call_target="tpu_custom_call" | custom-call | flops 4378853376 | bytes 3145728 | tf_op jit(solution)/shard_map/cells_12_4/pallas_call | solution.py:101
  49.5 3.5 %collective-permute-start.5 = (f32[48,256]{1,0:T(8,128)S(1)}, f32[48,256]{1,0:T(8,128)S(1)}, u32[]{:S(2)}, u32[]{:S(2)}) collective-permute-start(f32[48,256]{1,0:T(8,128)S(1)} %get-tuple-element.26), channel_id=1, source_target_pairs={{0,8},{8,16},{16,24},{24,32},{32,40},{40,48},{48,56},{56,64},{64,7... | collective-permute-start | bytes 147464 | tf_op jit(solution)/shard_map/ppermute | solution.py:289
  53.1 2.9 %cells_6_6.5.total_ref = f32[48,2048]{1,0:T(8,128)S(1)} custom-call(f32[16]{0:T(128)S(1)} %copy-done.8, s32[16,512]{1,0:T(8,128)S(1)} %copy-done.7, bf16[512,512]{1,0:T(8,128)(2,1)S(1)} %copy-done.6, bf16[48,2048]{1,0:T(8,128)(2,1)S(1)} %get-tuple-element.23.refs_2_.new_ref, f32[48,2048]{1,0:T(8,128)S(1)} %cells_0_6.5.refs_3_, ...), custom_call_target="tpu_custom_call" | custom-call | flops 5888802816 | bytes 3145728 | tf_op jit(solution)/shard_map/cells_6_6/pallas_call | solution.py:101
  57.2 3.5 %all-to-all-start = ((bf16[8,48,1024]{2,1,0:T(8,128)(2,1)}), bf16[8,48,1024]{2,1,0:T(8,128)(2,1)S(1)}, u32[]{:S(2)}, u32[]{:S(2)}) async-start(bf16[8,48,1024]{2,1,0:T(8,128)(2,1)} %bitcast.4), calls=%async_computation | async-start | bytes 1572864 | tf_op jit(solution)/shard_map/all_to_all | solution.py:293
  60.9 22.6 %all-to-all-done = bf16[8,48,1024]{2,1,0:T(8,128)(2,1)S(1)} async-done(((bf16[8,48,1024]{2,1,0:T(8,128)(2,1)}), bf16[8,48,1024]{2,1,0:T(8,128)(2,1)S(1)}, u32[]{:S(2)}, u32[]{:S(2)}) %all-to-all-start) | async-done | bytes 786464 | tf_op jit(solution)/shard_map/all_to_all | solution.py:293
  84.4 14.0 %all_to_all.20 = f32[16,6,384]{2,1,0:T(8,128)S(1)} all-to-all(f32[16,6,384]{2,1,0:T(8,128)S(1)} %gram.1), channel_id=1, replica_groups=mesh['z'=12,'yl'=4,'core'=2,'yh'=2,'x'=4] {'core','yl','yh'}, dimensions={0} | all-to-all | bytes 294912 | tf_op jit(solution)/shard_map/all_to_all | solution.py:293
  98.4 26.9 %all_to_all.21 = f32[12,6,384]{2,1,0:T(8,128)S(1)} all-to-all(f32[12,6,384]{2,1,0:T(8,128)S(1)} %broadcast_in_dim.7), channel_id=1, replica_groups=mesh['z'=12,'yl'=4,'core'=2,'yh'=2,'x'=4] {'z'}, dimensions={0} | all-to-all | bytes 221184 | tf_op jit(solution)/shard_map/all_to_all | solution.py:293
  125.3 16.9 %all_to_all.22 = f32[32,6,384]{2,1,0:T(8,128)S(1)} all-to-all(f32[32,6,384]{2,1,0:T(8,128)S(1)} %broadcast_in_dim.8), channel_id=1, replica_groups=mesh['z'=12,'yl'=4,'core'=2,'yh'=2,'x'=4] {'x','yl','yh'}, dimensions={0} | all-to-all | bytes 589824 | tf_op jit(solution)/shard_map/all_to_all | solution.py:293
  142.3 6.9 %collective-permute-start.6 = (f32[192,384]{1,0:T(8,128)S(1)}, f32[192,384]{1,0:T(8,128)S(1)}, u32[]{:S(2)}, u32[]{:S(2)}) collective-permute-start(f32[192,384]{1,0:T(8,128)S(1)} %reshape.13.here_ref), channel_id=1, source_target_pairs={{0,8},{8,0},{1,9},{9,1},{2,10},{10,2},{3,11},{11,3},{4,12},{12,4},... | collective-permute-start | bytes 884744 | tf_op jit(solution)/shard_map/ppermute | solution.py:308
  150.4 5.9 %rotate.1 = (bf16[48,1024]{1,0:T(8,128)(2,1)S(1)}, bf16[48,1024]{1,0:T(8,128)(2,1)S(1)}) custom-call(s32[3]{0:T(128)S(1)} %pad_add_fusion.side_ref, f32[192,384]{1,0:T(8,128)S(1)} %reshape.13.here_ref, f32[192,384]{1,0:T(8,128)S(1)} %collective-permute-done.6.there_ref, bf16[384,1024]{1,0:T(8,128)(2,1)S(1)} %bitcast.7), custom_call_target="tpu_custom_call" | custom-call | tf_op jit(solution)/shard_map/rotate/pallas_call | solution.py:275
  156.3 3.4 %collective-permute-start.7 = (bf16[48,1024]{1,0:T(8,128)(2,1)S(1)}, bf16[48,1024]{1,0:T(8,128)(2,1)S(1)}, u32[]{:S(2)}, u32[]{:S(2)}) collective-permute-start(bf16[48,1024]{1,0:T(8,128)(2,1)S(1)} %get-tuple-element.28), channel_id=1, source_target_pairs={{0,4},{4,0},{1,5},{5,1},{2,6},{6,2},{3,7},{7,3},{8,12},{12,8},{9,1... | collective-permute-start | bytes 294920 | tf_op jit(solution)/shard_map/ppermute | solution.py:308
  159.7 8.6 %collective-permute-done.7 = bf16[48,1024]{1,0:T(8,128)(2,1)S(1)} collective-permute-done((bf16[48,1024]{1,0:T(8,128)(2,1)S(1)}, bf16[48,1024]{1,0:T(8,128)(2,1)S(1)}, u32[]{:S(2)}, u32[]{:S(2)}) %collective-permute-start.7) | collective-permute-done | bytes 98336 | tf_op jit(solution)/shard_map/ppermute | solution.py:308
  (37 shorter events, 9.8 us)
Async XLA Ops:
  0.0 0.9 copy-start
  0.9 0.7 copy-start.3
  1.6 12.6 %copy-start.1 = (bf16[48,2048]{1,0:T(8,128)(2,1)S(1)}, bf16[48,2048]{1,0:T(8,128)(2,1)}, u32[]{:S(2)}) copy-start(bf16[48,2048]{1,0:T(8,128)(2,1)} %refs_0_.16) | copy-start | bytes 589828
  1.6 12.6 %copy-start.8 = (f32[16]{0:T(128)S(1)}, f32[16]{0:T(128)}, u32[]{:S(2)}) copy-start(f32[16]{0:T(128)} %scale_ref.17) | copy-start | bytes 196
  1.8 17.1 %collective-permute-start = (bf16[48,256]{1,0:T(8,128)(2,1)S(1)}, bf16[48,256]{1,0:T(8,128)(2,1)S(1)}, u32[]{:S(2)}, u32[]{:S(2)}) collective-permute-start(bf16[48,256]{1,0:T(8,128)(2,1)S(1)} %edge.1), channel_id=1, source_target_pairs={{8,0},{16,8},{24,16},{32,24},{40,32},{48,40},{56,48},{64,56},{72,6... | collective-permute-start | bytes 73736 | tf_op jit(solution)/shard_map/ppermute | solution.py:289
  14.2 1.0 copy-start.5
  15.3 0.8 copy-start.7
  21.4 4.9 %collective-permute-start.1 = (f32[48,256]{1,0:T(8,128)S(1)}, f32[48,256]{1,0:T(8,128)S(1)}, u32[]{:S(2)}, u32[]{:S(2)}) collective-permute-start(f32[48,256]{1,0:T(8,128)S(1)} %get-tuple-element.18), channel_id=1, source_target_pairs={{0,8},{8,16},{16,24},{24,32},{32,40},{40,48},{48,56},{56,64},{64,7... | collective-permute-start | bytes 147464 | tf_op jit(solution)/shard_map/ppermute | solution.py:289
  23.4 3.0 %copy-start.2 = (f32[2048]{0:T(1024)S(1)}, f32[2048]{0:T(1024)}, u32[]{:S(2)}) copy-start(f32[2048]{0:T(1024)} %param.11) | copy-start | bytes 24580
  26.3 0.7 copy-start.4
  26.3 3.6 %copy-start.6 = (bf16[512,512]{1,0:T(8,128)(2,1)S(1)}, bf16[512,512]{1,0:T(8,128)(2,1)}, u32[]{:S(2)}) copy-start(bf16[512,512]{1,0:T(8,128)(2,1)} %refs_1_.17) | copy-start | bytes 1572868
  27.5 5.3 %collective-permute-start.2 = (bf16[48,256]{1,0:T(8,128)(2,1)S(1)}, bf16[48,256]{1,0:T(8,128)(2,1)S(1)}, u32[]{:S(2)}, u32[]{:S(2)}) collective-permute-start(bf16[48,256]{1,0:T(8,128)(2,1)S(1)} %get-tuple-element.20), channel_id=1, source_target_pairs={{8,0},{16,8},{24,16},{32,24},{40,32},{48,40},{56,48},{64,56},{72,6... | collective-permute-start | bytes 73736 | tf_op jit(solution)/shard_map/ppermute | solution.py:289
  35.3 6.1 %collective-permute-start.3 = (f32[48,256]{1,0:T(8,128)S(1)}, f32[48,256]{1,0:T(8,128)S(1)}, u32[]{:S(2)}, u32[]{:S(2)}) collective-permute-start(f32[48,256]{1,0:T(8,128)S(1)} %get-tuple-element.22), channel_id=1, source_target_pairs={{0,8},{8,16},{16,24},{24,32},{32,40},{40,48},{48,56},{56,64},{64,7... | collective-permute-start | bytes 147464 | tf_op jit(solution)/shard_map/ppermute | solution.py:289
  42.0 5.1 %collective-permute-start.4 = (bf16[48,256]{1,0:T(8,128)(2,1)S(1)}, bf16[48,256]{1,0:T(8,128)(2,1)S(1)}, u32[]{:S(2)}, u32[]{:S(2)}) collective-permute-start(bf16[48,256]{1,0:T(8,128)(2,1)S(1)} %get-tuple-element.24), channel_id=1, source_target_pairs={{8,0},{16,8},{24,16},{32,24},{40,32},{48,40},{56,48},{64,56},{72,6... | collective-permute-start | bytes 73736 | tf_op jit(solution)/shard_map/ppermute | solution.py:289
  49.5 6.5 %collective-permute-start.5 = (f32[48,256]{1,0:T(8,128)S(1)}, f32[48,256]{1,0:T(8,128)S(1)}, u32[]{:S(2)}, u32[]{:S(2)}) collective-permute-start(f32[48,256]{1,0:T(8,128)S(1)} %get-tuple-element.26), channel_id=1, source_target_pairs={{0,8},{8,16},{16,24},{24,32},{32,40},{40,48},{48,56},{56,64},{64,7... | collective-permute-start | bytes 147464 | tf_op jit(solution)/shard_map/ppermute | solution.py:289
  57.2 26.2 %all-to-all-start = ((bf16[8,48,1024]{2,1,0:T(8,128)(2,1)}), bf16[8,48,1024]{2,1,0:T(8,128)(2,1)S(1)}, u32[]{:S(2)}, u32[]{:S(2)}) async-start(bf16[8,48,1024]{2,1,0:T(8,128)(2,1)} %bitcast.4), calls=%async_computation | async-start | bytes 1572864 | tf_op jit(solution)/shard_map/all_to_all | solution.py:293
  142.3 8.1 %collective-permute-start.6 = (f32[192,384]{1,0:T(8,128)S(1)}, f32[192,384]{1,0:T(8,128)S(1)}, u32[]{:S(2)}, u32[]{:S(2)}) collective-permute-start(f32[192,384]{1,0:T(8,128)S(1)} %reshape.13.here_ref), channel_id=1, source_target_pairs={{0,8},{8,0},{1,9},{9,1},{2,10},{10,2},{3,11},{11,3},{4,12},{12,4},... | collective-permute-start | bytes 884744 | tf_op jit(solution)/shard_map/ppermute | solution.py:308
  156.3 12.0 %collective-permute-start.7 = (bf16[48,1024]{1,0:T(8,128)(2,1)S(1)}, bf16[48,1024]{1,0:T(8,128)(2,1)S(1)}, u32[]{:S(2)}, u32[]{:S(2)}) collective-permute-start(bf16[48,1024]{1,0:T(8,128)(2,1)S(1)} %get-tuple-element.28), channel_id=1, source_target_pairs={{0,4},{4,0},{1,5},{5,1},{2,6},{6,2},{3,7},{7,3},{8,12},{12,8},{9,1... | collective-permute-start | bytes 294920 | tf_op jit(solution)/shard_map/ppermute | solution.py:308
